TPU v7x, 32 devices: a whole 2x2x4 slice. The times are simulated.
32 devices in a mesh: dp: 4 (over y, x), mp: 8 (over z, core).
Axes of the slice: x: 2, y: 2, z: 4, core: 2. Of those that a mesh axis runs over, the one named last changes fastest.
Arguments:
- residual_in: bfloat16 [512, 3584], P('dp', 'mp'), may hold values from -6 to 6
- pre_gain: float32 [3584], replicated, may hold values from 0.5 to 1.5
- post_gain: float32 [3584], replicated, may hold values from 0.5 to 1.5
- w_gate: bfloat16 [3584, 14336], P(None, 'mp'), may hold values from -0.09375 to 0.09375
- w_up: bfloat16 [3584, 14336], P(None, 'mp'), may hold values from -0.09375 to 0.09375
- w_down: bfloat16 [14336, 3584], P('mp'), may hold values from -0.046875 to 0.046875
- w_enc: bfloat16 [3584, 16384], P(None, ('dp', 'mp')), may hold values from -0.09375 to 0.09375
- b_enc: float32 [16384], P(('dp', 'mp')), may hold values from -2.5 to 2.5
- threshold: float32 [16384], P(('dp', 'mp')), may hold values from 0.1 to 1
- w_dec: bfloat16 [16384, 3584], P(('dp', 'mp')), may hold values from -0.046875 to 0.046875
- b_dec: float32 [3584], replicated, may hold values from -1.5 to 1.5
Outputs:
- loss_value: float32 [], replicated
- d_w_enc: bfloat16 [3584, 16384], P(None, ('dp', 'mp'))
- d_w_dec: bfloat16 [16384, 3584], P(('dp', 'mp'))
- d_b_enc: float32 [16384], P(('dp', 'mp'))
- d_threshold: float32 [16384], P(('dp', 'mp'))
- d_b_dec: float32 [3584], replicated
All inputs are finite; a program needn't handle non-finite values.
Results may differ from a plain program's by a relative error of at most 0.014.
The roundings to bfloat16 on the way count: a program that leaves them out, or rounds other values in their place, can miss the bound.
Values may be sent and summed in bfloat16 or wider, within the bound.
No kernel may reach another device: no remote copies, remote signals or barrier semaphores. Data moves between devices by JAX's collectives and lax.ppermute only.
A program may use at most 128 MiB of HBM per device.

v0:
```python
import functools

import jax
import jax.numpy as jnp
from jax import lax
from jax.experimental import pallas as pl
from jax.experimental.pallas import tpu as pltpu
from jax.sharding import PartitionSpec as P


norm_eps = 1e-06
gate_band = 0.1
sparsity_coef = 0.05


f32 = jnp.float32
bf16 = jnp.bfloat16
both = ("dp", "mp")


def dot(left, right, left_dim, right_dim):
    return lax.dot_general(
        left, right, (((left_dim,), (right_dim,)), ((), ())), preferred_element_type=f32
    )


def finish(n_parts, entries, thr_ref, w_dec_ref, *rest):
    pairs = [rest[2 * i : 2 * i + 2] for i in range(3 + 2 * n_parts)]
    pre_refs, partial_refs, feat_refs = pairs[:3]
    layer_refs, err_refs = pairs[3 : 3 + n_parts], pairs[3 + n_parts :]
    wenc_ref, wdec_ref, gthr_ref, gbenc_ref, gbdec_ref, loss_ref, buffer, sems = rest[-8:]
    span = err_refs[0][0].shape[1]
    n_slots = buffer.shape[0]
    step = buffer.shape[1]
    copies = []

    def send(value, target):
        index = len(copies)
        slot = index % n_slots
        if index >= n_slots:
            copies[index - n_slots].wait()
        rows, cols = value.shape
        block = buffer.at[slot, pl.ds(0, rows), pl.ds(0, cols)]
        block[...] = value.astype(bf16)
        copy = pltpu.make_async_copy(block, target, sems.at[slot])
        copy.start()
        copies.append(copy)

    def grad_wdec(i):
        for low in range(0, span, step):
            size = min(step, span - low)
            value = sum(
                dot(feat[...], err[:, low : low + size], 0, 0)
                for feat, err in zip(feat_refs, err_refs[i])
            )
            send(value, wdec_ref.at[:, pl.ds(i * span + low, size)])
            ones = jnp.ones((8, err_refs[i][0].shape[0]), bf16)
            gbdec_ref[:, i * span + low : i * span + low + size] = sum(
                dot(ones, err[:, low : low + size], 1, 0)[:1] for err in err_refs[i]
            )

    for i in range(n_parts - 1):
        grad_wdec(i)

    weight = w_dec_ref[:, (n_parts - 1) * span :]
    grads, sums_thr, sums_benc = [], 0.0, 0.0
    for pre_ref, partial_ref, err_ref in zip(pre_refs, partial_refs, err_refs[-1]):
        grad_feat = partial_ref[...] + dot(err_ref[:, :span], weight, 1, 1)
        pre = pre_ref[...]
        soft = jax.nn.sigmoid((pre - thr_ref[...]) / gate_band)
        slope = soft * (1.0 - soft) / gate_band
        side_term = (grad_feat * pre + sparsity_coef) * slope
        grad = grad_feat * soft + side_term
        sums_thr = sums_thr - jnp.sum(side_term, axis=0, keepdims=True)
        sums_benc = sums_benc + jnp.sum(grad, axis=0, keepdims=True)
        grads.append(grad.astype(bf16))
    shares = sum(
        jnp.sum(err_ref[:, span:].astype(f32), axis=0, keepdims=True)
        for err_ref in err_refs[-1]
    )
    loss_ref[0, 0] = jnp.sum(shares) / entries
    gthr_ref[...] = sums_thr
    gbenc_ref[...] = sums_benc
    for i, layers in enumerate(layer_refs):
        for low in range(0, span, step):
            size = min(step, span - low)
            value = sum(
                dot(layer[:, low : low + size], grad, 0, 0)
                for layer, grad in zip(layers, grads)
            )
            send(value, wenc_ref.at[pl.ds(i * span + low, size), :])
    grad_wdec(n_parts - 1)
    for copy in copies[-n_slots:]:
        copy.wait()


def program(n_dp, n_mp):
    n_z = n_mp // 2
    everyone = [(d, m) for d in range(n_dp) for m in range(n_mp)]

    bits_of = lambda count: [1 << i for i in range((count - 1).bit_length())]
    z_steps = [(0, bit) for bit in bits_of(n_z)]
    dp_steps = [(bit, 0) for bit in bits_of(n_dp)]
    orders = (z_steps + dp_steps, z_steps[::-1] + dp_steps[::-1])
    steps = len(orders[0])

    def other_core(value):
        return lax.ppermute(
            value, both, [(d * n_mp + m, d * n_mp + (m ^ 1)) for d, m in everyone]
        )

    def exchange(value, step):
        pairs = []
        for d, m in everyone:
            dp_bits, z_bits = orders[m % 2][step]
            pairs.append((d * n_mp + m, (d ^ dp_bits) * n_mp + (m ^ (2 * z_bits))))
        return lax.ppermute(value, both, pairs)

    def gather(rows):
        for step in range(steps):
            got = exchange(rows, step)
            rows = jnp.concatenate([rows, got], axis=0)
        return rows

    def scatter(total, count):
        for step in reversed(range(count)):
            cut = total.shape[0] // 2
            give = total[cut:].astype(bf16)
            got = exchange(give, step)
            total = total[:cut] + got.astype(f32)
        return total

    def whole_step(
        residual_in, pre_gain, post_gain, w_gate, w_up, w_down, w_enc, b_enc, threshold, w_dec, b_dec
    ):
        tokens, width = residual_in.shape[0] * n_dp, w_gate.shape[0]
        at_mp = lax.axis_index("mp")
        at_z, at_core = at_mp // 2, at_mp % 2
        count = residual_in.shape[0] // n_mp

        def columns(cuts):
            span = width // cuts
            return [slice(i * span, (i + 1) * span) for i in range(cuts)]

        full_rows = lax.all_gather(residual_in, "mp", axis=1, tiled=True)
        slot = jnp.arange(n_z)
        turned = sum(
            ((slot >> i) & 1) << (len(z_steps) - 1 - i) for i in range(len(z_steps))
        )
        straight = jnp.where(at_core == 0, slot, turned)
        crossed = jnp.where(at_core == 0, turned, slot)
        owner = jnp.concatenate(
            [2 * (at_z ^ straight) + at_core, 2 * (at_z ^ crossed) + 1 - at_core]
        )
        source = (owner[:, None] * count + jnp.arange(count)[None, :]).reshape(-1)
        pick = (source[:, None] == jnp.arange(source.shape[0])[None, :]).astype(bf16)
        full_rows = dot(pick, full_rows, 1, 0).astype(bf16)

        resid_wide = full_rows.astype(f32)
        normed = (
            resid_wide
            * lax.rsqrt(jnp.mean(resid_wide * resid_wide, axis=1, keepdims=True) + norm_eps)
            * pre_gain[None, :]
        ).astype(bf16)
        gate_out = dot(normed, w_gate, 1, 0)
        up_out = dot(normed, w_up, 1, 0)
        hidden = (jax.nn.gelu(gate_out, approximate=True) * up_out).astype(bf16)
        hidden = lax.optimization_barrier(hidden)
        half = hidden.shape[0] // 2
        blocks = []
        for cols in columns(2):
            part = dot(hidden, w_down[:, cols], 1, 0)
            mine = part[:half] + other_core(part[half:].astype(bf16)).astype(f32)
            blocks.append(scatter(mine, len(z_steps)))
        block = jnp.concatenate(blocks, axis=1)
        layer_own = (
            resid_wide[:count]
            + block
            * lax.rsqrt(jnp.mean(block * block, axis=1, keepdims=True) + norm_eps)
            * post_gain[None, :]
        ).astype(bf16)

        layer_out = []
        for cols in columns(2):
            near = gather(layer_own[:, cols])
            layer_out.append((near, other_core(near)))
        sides = range(2)

        def over(parts, weight, dim, side, leave=0):
            return sum(
                dot(part[side], weight(cols), 1, dim)
                for part, cols in list(zip(parts, columns(len(parts))))[: len(parts) - leave]
            )

        pre_act = [
            over(layer_out, lambda cols: w_enc[cols, :], 0, side) + b_enc[None, :]
            for side in sides
        ]
        soft = [jax.nn.sigmoid((pre - threshold[None, :]) / gate_band) for pre in pre_act]
        feat = [(pre * open_).astype(bf16) for pre, open_ in zip(pre_act, soft)]
        lanes = 128

        def fold(row):
            return sum(row[:, i : i + lanes] for i in range(0, row.shape[1], lanes))

        open_total = sum(
            fold(jnp.sum(open_, axis=0, keepdims=True)) for open_ in soft
        )
        error_own = []
        for cols in columns(2):
            far = other_core(dot(feat[1], w_dec[:, cols], 1, 0).astype(bf16))
            mine = dot(feat[0], w_dec[:, cols], 1, 0) + far.astype(f32)
            recon = scatter(mine, steps)
            error_own.append(recon + b_dec[None, cols] - layer_own[:, cols].astype(f32))

        rest = 0.5 * sum(
            fold(jnp.sum(error * error, axis=0, keepdims=True)) for error in error_own
        ) + sparsity_coef * open_total
        row = jnp.arange(count)[:, None]
        extra = jnp.zeros((count, lanes), f32)
        for i in range(3):
            term = lax.reduce_precision(rest, 8, 7)
            extra = jnp.where(row == i, term, extra)
            rest = rest - term
        extra = extra.astype(bf16)

        err_all = []
        for i, error in enumerate(error_own):
            rows = error.astype(bf16)
            if i == len(error_own) - 1:
                rows = jnp.concatenate([rows, extra], axis=1)
            near = gather(rows)
            err_all.append((near, other_core(near)))

        vmem = pl.BlockSpec(memory_space=pltpu.VMEM)
        hbm = pl.BlockSpec(memory_space=pl.ANY)
        features = w_enc.shape[1]
        pairs = [pre_act]
        pairs.append(
            [over(err_all, lambda cols: w_dec[:, cols], 1, side, 1) for side in sides]
        )
        pairs += [feat] + layer_out + err_all
        operands = [threshold[None, :], w_dec] + [part for pair in pairs for part in pair]
        n_slots = 4
        grad_wenc, grad_wdec, grad_thresh, grad_benc, grad_bdec, shares = pl.pallas_call(
            functools.partial(finish, len(err_all), float(tokens * width)),
            out_shape=(
                jax.ShapeDtypeStruct((width, features), bf16),
                jax.ShapeDtypeStruct((features, width), bf16),
                jax.ShapeDtypeStruct((1, features), f32),
                jax.ShapeDtypeStruct((1, features), f32),
                jax.ShapeDtypeStruct((1, width), f32),
                jax.ShapeDtypeStruct((1, 1), f32),
            ),
            in_specs=[vmem] * len(operands),
            out_specs=(hbm, hbm, vmem, vmem, vmem, pl.BlockSpec(memory_space=pltpu.SMEM)),
            scratch_shapes=[
                pltpu.VMEM((n_slots, 512, 512), bf16),
                pltpu.SemaphoreType.DMA((n_slots,)),
            ],
            compiler_params=pltpu.CompilerParams(vmem_limit_bytes=40 * 2**20),
            name="finish",
        )(*operands)
        grad_thresh, grad_benc, grad_bdec = grad_thresh[0], grad_benc[0], grad_bdec[0]
        loss_value = shares[0, 0]
        return (loss_value, grad_wenc, grad_wdec, grad_benc, grad_thresh, grad_bdec)

    return whole_step


def solution(mesh):
    placed = (
        P("dp", "mp"),
        P(),
        P(),
        P(None, "mp"),
        P(None, "mp"),
        P("mp", None),
        P(None, both),
        P(both),
        P(both),
        P(both, None),
        P(),
    )
    return jax.shard_map(
        program(mesh.shape["dp"], mesh.shape["mp"]),
        mesh=mesh,
        in_specs=placed,
        out_specs=(P(), P(None, both), P(both, None), P(both), P(both), P()),
        check_vma=False,
    )
```

profile of v0, /device:TPU:0, one launch (start us, length us, event | category | flops | bytes accessed | tf_op | source)
XLA Modules:
  0.0 178.3 jit_solution(3843775621993931149)
XLA Ops:
  0.9 17.9 %all_gather.3 = bf16[128,3584]{0,1:T(8,128)(2,1)S(1)} all-gather(bf16[128,448]{0,1:T(8,128)(2,1)} %param.11), channel_id=1, replica_groups=mesh['dp'=4,'mp'=8] {'mp'}, dimensions={1}, use_global_device_ids=true | all-gather | bytes 1032192 | tf_op jit(solution)/shard_map/all_gather | solution.py:145
  19.5 6.9 %fusion.71 = f32[128,1792]{1,0:T(8,128)S(1)} fusion(bf16[3584,1792]{1,0:T(8,128)(2,1)} %param.14, f32[128,3584]{1,0:T(8,128)S(1)} %get-tuple-element.40, f32[3584]{0:T(1024)S(1)} %copy-done.2, f32[128]{0:T(128)S(1)} %add_rsqrt_fusion.1), kind=kOutput, calls=%fused_computation.189 | convolution fusion | flops 1645543424 | bytes 15612416 | tf_op jit(solution)/shard_map/dot_general | solution.py:22
  27.3 2.2 %fusion.5 = bf16[128,1792]{1,0:T(8,128)(2,1)S(1)} fusion(bf16[3584,1792]{1,0:T(8,128)(2,1)S(1)} %bitcast.29, f32[128,1792]{1,0:T(8,128)S(1)} %fusion.71, f32[128,3584]{1,0:T(8,128)S(1)} %get-tuple-element.40, f32[3584]{0:T(1024)S(1)} %copy-done.2, f32[128]{0:T(128)S(1)} %add_rsqrt_fusion.1), kind=kOutput, calls=%fused_computation.9 | convolution fusion | flops 1647837184 | bytes 16071168 | tf_op jit(solution)/shard_map/dot_general | solution.py:22
  36.9 2.7 %collective-permute-done.4 = bf16[32,1792]{1,0:T(8,128)(2,1)S(1)} collective-permute-done((bf16[32,1792]{1,0:T(8,128)(2,1)S(1)}, bf16[32,1792]{1,0:T(8,128)(2,1)S(1)}, u32[]{:S(2)}, u32[]{:S(2)}) %collective-permute-start.4) | collective-permute-done | bytes 114720 | tf_op jit(solution)/shard_map/ppermute | solution.py:117
  39.7 3.0 %collective-permute-start.5 = (bf16[16,1792]{1,0:T(8,128)(2,1)S(1)}, bf16[16,1792]{1,0:T(8,128)(2,1)S(1)}, u32[]{:S(2)}, u32[]{:S(2)}) collective-permute-start(bf16[16,1792]{1,0:T(8,128)(2,1)S(1)} %slice.662), channel_id=1, source_target_pairs={{0,2},{1,5},{2,0},{3,7},{4,6},{5,1},{6,4},{7,3},{8,10},{9,13},{10,... | collective-permute-start | bytes 172040 | tf_op jit(solution)/shard_map/ppermute | solution.py:117
  51.5 2.9 %collective-permute-start.7 = (bf16[32,1792]{1,0:T(8,128)(2,1)S(1)}, bf16[32,1792]{1,0:T(8,128)(2,1)S(1)}, u32[]{:S(2)}, u32[]{:S(2)}) collective-permute-start(bf16[32,1792]{1,0:T(8,128)(2,1)S(1)} %pad_maximum_fusion.10), channel_id=1, source_target_pairs={{0,4},{1,3},{2,6},{3,1},{4,0},{5,7},{6,2},{7,5},{8,12},{9,11},{10,... | collective-permute-start | bytes 344072 | tf_op jit(solution)/shard_map/ppermute | solution.py:117
  54.4 2.4 %collective-permute-start.11 = (bf16[32,1792]{1,0:T(8,128)(2,1)S(1)}, bf16[32,1792]{1,0:T(8,128)(2,1)S(1)}, u32[]{:S(2)}, u32[]{:S(2)}) collective-permute-start(bf16[32,1792]{1,0:T(8,128)(2,1)S(1)} %pad_maximum_fusion.11), channel_id=1, source_target_pairs={{0,4},{1,3},{2,6},{3,1},{4,0},{5,7},{6,2},{7,5},{8,12},{9,11},{10,... | collective-permute-start | bytes 344072 | tf_op jit(solution)/shard_map/ppermute | solution.py:117
  58.9 3.0 %collective-permute-done.11 = bf16[32,1792]{1,0:T(8,128)(2,1)S(1)} collective-permute-done((bf16[32,1792]{1,0:T(8,128)(2,1)S(1)}, bf16[32,1792]{1,0:T(8,128)(2,1)S(1)}, u32[]{:S(2)}, u32[]{:S(2)}) %collective-permute-start.11) | collective-permute-done | bytes 114720 | tf_op jit(solution)/shard_map/ppermute | solution.py:117
  63.5 7.0 %collective-permute-done.12 = bf16[64,1792]{1,0:T(8,128)(2,1)S(1)} collective-permute-done((bf16[64,1792]{1,0:T(8,128)(2,1)S(1)}, bf16[64,1792]{1,0:T(8,128)(2,1)S(1)}, u32[]{:S(2)}, u32[]{:S(2)}) %collective-permute-start.12) | collective-permute-done | bytes 229408 | tf_op jit(solution)/shard_map/ppermute | solution.py:117
  72.7 6.3 %collective-permute-done.13 = bf16[128,1792]{1,0:T(8,128)(2,1)S(1)} collective-permute-done((bf16[128,1792]{1,0:T(8,128)(2,1)S(1)}, bf16[128,1792]{1,0:T(8,128)(2,1)S(1)}, u32[]{:S(2)}, u32[]{:S(2)}) %collective-permute-start.13) | collective-permute-done | bytes 458784 | tf_op jit(solution)/shard_map/ppermute | solution.py:117
  79.2 4.8 %collective-permute-done.9 = bf16[128,1792]{1,0:T(8,128)(2,1)S(1)} collective-permute-done((bf16[128,1792]{1,0:T(8,128)(2,1)S(1)}, bf16[128,1792]{1,0:T(8,128)(2,1)S(1)}, u32[]{:S(2)}, u32[]{:S(2)}) %collective-permute-start.9) | collective-permute-done | bytes 458784 | tf_op jit(solution)/shard_map/ppermute | solution.py:117
  96.2 5.7 %collective-permute-done.17 = bf16[128,1792]{1,0:T(8,128)(2,1)S(1)} collective-permute-done((bf16[128,1792]{1,0:T(8,128)(2,1)S(1)}, bf16[128,1792]{1,0:T(8,128)(2,1)S(1)}, u32[]{:S(2)}, u32[]{:S(2)}) %collective-permute-start.17) | collective-permute-done | bytes 458784 | tf_op jit(solution)/shard_map/ppermute | solution.py:117
  103.5 5.8 %collective-permute-done.27 = bf16[128,1792]{1,0:T(8,128)(2,1)S(1)} collective-permute-done((bf16[128,1792]{1,0:T(8,128)(2,1)S(1)}, bf16[128,1792]{1,0:T(8,128)(2,1)S(1)}, u32[]{:S(2)}, u32[]{:S(2)}) %collective-permute-start.27) | collective-permute-done | bytes 458784 | tf_op jit(solution)/shard_map/ppermute | solution.py:117
  111.1 4.4 %collective-permute-done.28 = bf16[64,1792]{1,0:T(8,128)(2,1)S(1)} collective-permute-done((bf16[64,1792]{1,0:T(8,128)(2,1)S(1)}, bf16[64,1792]{1,0:T(8,128)(2,1)S(1)}, u32[]{:S(2)}, u32[]{:S(2)}) %collective-permute-start.28) | collective-permute-done | bytes 229408 | tf_op jit(solution)/shard_map/ppermute | solution.py:117
  115.7 3.5 %collective-permute-done.19 = bf16[32,1792]{1,0:T(8,128)(2,1)S(1)} collective-permute-done((bf16[32,1792]{1,0:T(8,128)(2,1)S(1)}, bf16[32,1792]{1,0:T(8,128)(2,1)S(1)}, u32[]{:S(2)}, u32[]{:S(2)}) %collective-permute-start.19) | collective-permute-done | bytes 114720 | tf_op jit(solution)/shard_map/ppermute | solution.py:117
  119.3 3.9 %collective-permute-done.29 = bf16[32,1792]{1,0:T(8,128)(2,1)S(1)} collective-permute-done((bf16[32,1792]{1,0:T(8,128)(2,1)S(1)}, bf16[32,1792]{1,0:T(8,128)(2,1)S(1)}, u32[]{:S(2)}, u32[]{:S(2)}) %collective-permute-start.29) | collective-permute-done | bytes 114720 | tf_op jit(solution)/shard_map/ppermute | solution.py:117
  124.4 3.4 %collective-permute-done.30 = bf16[16,1792]{1,0:T(8,128)(2,1)S(1)} collective-permute-done((bf16[16,1792]{1,0:T(8,128)(2,1)S(1)}, bf16[16,1792]{1,0:T(8,128)(2,1)S(1)}, u32[]{:S(2)}, u32[]{:S(2)}) %collective-permute-start.30) | collective-permute-done | bytes 57376 | tf_op jit(solution)/shard_map/ppermute | solution.py:117
  135.3 5.2 %collective-permute-done.22 = bf16[32,1792]{1,0:T(8,128)(2,1)S(1)} collective-permute-done((bf16[32,1792]{1,0:T(8,128)(2,1)S(1)}, bf16[32,1792]{1,0:T(8,128)(2,1)S(1)}, u32[]{:S(2)}, u32[]{:S(2)}) %collective-permute-start.22) | collective-permute-done | bytes 114720 | tf_op jit(solution)/shard_map/ppermute | solution.py:117
  140.6 2.7 %collective-permute-start.23 = (bf16[64,1792]{1,0:T(8,128)(2,1)S(1)}, bf16[64,1792]{1,0:T(8,128)(2,1)S(1)}, u32[]{:S(2)}, u32[]{:S(2)}) collective-permute-start(bf16[64,1792]{1,0:T(8,128)(2,1)S(1)} %pad_maximum_fusion.8), channel_id=1, source_target_pairs={{0,8},{1,17},{2,10},{3,19},{4,12},{5,21},{6,14},{7,23},{8,0},{9,25... | collective-permute-start | bytes 688136 | tf_op jit(solution)/shard_map/ppermute | solution.py:117
  144.6 5.1 %collective-permute-done.23 = bf16[64,1792]{1,0:T(8,128)(2,1)S(1)} collective-permute-done((bf16[64,1792]{1,0:T(8,128)(2,1)S(1)}, bf16[64,1792]{1,0:T(8,128)(2,1)S(1)}, u32[]{:S(2)}, u32[]{:S(2)}) %collective-permute-start.23) | collective-permute-done | bytes 229408 | tf_op jit(solution)/shard_map/ppermute | solution.py:117
  151.4 2.9 %collective-permute-done.33 = bf16[64,1920]{1,0:T(8,128)(2,1)S(1)} collective-permute-done((bf16[64,1920]{1,0:T(8,128)(2,1)S(1)}, bf16[64,1920]{1,0:T(8,128)(2,1)S(1)}, u32[]{:S(2)}, u32[]{:S(2)}) %collective-permute-start.33) | collective-permute-done | bytes 245792 | tf_op jit(solution)/shard_map/ppermute | solution.py:117
  156.0 2.3 %collective-permute-done.24 = bf16[128,1792]{1,0:T(8,128)(2,1)S(1)} collective-permute-done((bf16[128,1792]{1,0:T(8,128)(2,1)S(1)}, bf16[128,1792]{1,0:T(8,128)(2,1)S(1)}, u32[]{:S(2)}, u32[]{:S(2)}) %collective-permute-start.24) | collective-permute-done | bytes 458784 | tf_op jit(solution)/shard_map/ppermute | solution.py:117
  158.5 5.1 %collective-permute-done.34 = bf16[128,1920]{1,0:T(8,128)(2,1)S(1)} collective-permute-done((bf16[128,1920]{1,0:T(8,128)(2,1)S(1)}, bf16[128,1920]{1,0:T(8,128)(2,1)S(1)}, u32[]{:S(2)}, u32[]{:S(2)}) %collective-permute-start.34) | collective-permute-done | bytes 491552 | tf_op jit(solution)/shard_map/ppermute | solution.py:117
  166.3 11.4 %finish.1 = (bf16[3584,512]{1,0:T(8,128)(2,1)}, bf16[512,3584]{1,0:T(8,128)(2,1)}, f32[1,512]{1,0:T(1,128)}, f32[1,512]{1,0:T(1,128)}, f32[1,3584]{1,0:T(1,128)S(1)}, /*index=5*/f32[1,1]{1,0:T(1,128)}) custom-call(f32[1,512]{1,0:T(1,128)S(1)} %bitcast.27, bf16[512,3584]{1,0:T(8,128)(2,1)S(1)} %copy-done, f32[256,512]{1,0:T(8,128)S(1)} %get-tuple-element.41.rest_0_, ...), custom_call_target="tpu_custom_call" | custom-call | tf_op jit(solution)/shard_map/finish/pallas_call | solution.py:245
  (172 shorter events, 56.5 us)
Async XLA Ops:
  33.8 5.9 %collective-permute-start.4 = (bf16[32,1792]{1,0:T(8,128)(2,1)S(1)}, bf16[32,1792]{1,0:T(8,128)(2,1)S(1)}, u32[]{:S(2)}, u32[]{:S(2)}) collective-permute-start(bf16[32,1792]{1,0:T(8,128)(2,1)S(1)} %slice.658), channel_id=1, source_target_pairs={{0,4},{1,3},{2,6},{3,1},{4,0},{5,7},{6,2},{7,5},{8,12},{9,11},{10,... | collective-permute-start | bytes 344072 | tf_op jit(solution)/shard_map/ppermute | solution.py:117
  35.1 7.6 %collective-permute-start.1 = (bf16[32,1792]{1,0:T(8,128)(2,1)S(1)}, bf16[32,1792]{1,0:T(8,128)(2,1)S(1)}, u32[]{:S(2)}, u32[]{:S(2)}) collective-permute-start(bf16[32,1792]{1,0:T(8,128)(2,1)S(1)} %slice.659), channel_id=1, source_target_pairs={{0,4},{1,3},{2,6},{3,1},{4,0},{5,7},{6,2},{7,5},{8,12},{9,11},{10,... | collective-permute-start | bytes 344072 | tf_op jit(solution)/shard_map/ppermute | solution.py:117
  39.7 5.2 %collective-permute-start.5 = (bf16[16,1792]{1,0:T(8,128)(2,1)S(1)}, bf16[16,1792]{1,0:T(8,128)(2,1)S(1)}, u32[]{:S(2)}, u32[]{:S(2)}) collective-permute-start(bf16[16,1792]{1,0:T(8,128)(2,1)S(1)} %slice.662), channel_id=1, source_target_pairs={{0,2},{1,5},{2,0},{3,7},{4,6},{5,1},{6,4},{7,3},{8,10},{9,13},{10,... | collective-permute-start | bytes 172040 | tf_op jit(solution)/shard_map/ppermute | solution.py:117
  49.1 5.3 %collective-permute-start.10 = (bf16[16,1792]{1,0:T(8,128)(2,1)S(1)}, bf16[16,1792]{1,0:T(8,128)(2,1)S(1)}, u32[]{:S(2)}, u32[]{:S(2)}) collective-permute-start(bf16[16,1792]{1,0:T(8,128)(2,1)S(1)} %get-tuple-element.32), channel_id=1, source_target_pairs={{0,2},{1,5},{2,0},{3,7},{4,6},{5,1},{6,4},{7,3},{8,10},{9,13},{10,... | collective-permute-start | bytes 172040 | tf_op jit(solution)/shard_map/ppermute | solution.py:117
  51.5 5.8 %collective-permute-start.7 = (bf16[32,1792]{1,0:T(8,128)(2,1)S(1)}, bf16[32,1792]{1,0:T(8,128)(2,1)S(1)}, u32[]{:S(2)}, u32[]{:S(2)}) collective-permute-start(bf16[32,1792]{1,0:T(8,128)(2,1)S(1)} %pad_maximum_fusion.10), channel_id=1, source_target_pairs={{0,4},{1,3},{2,6},{3,1},{4,0},{5,7},{6,2},{7,5},{8,12},{9,11},{10,... | collective-permute-start | bytes 344072 | tf_op jit(solution)/shard_map/ppermute | solution.py:117
  54.4 7.5 %collective-permute-start.11 = (bf16[32,1792]{1,0:T(8,128)(2,1)S(1)}, bf16[32,1792]{1,0:T(8,128)(2,1)S(1)}, u32[]{:S(2)}, u32[]{:S(2)}) collective-permute-start(bf16[32,1792]{1,0:T(8,128)(2,1)S(1)} %pad_maximum_fusion.11), channel_id=1, source_target_pairs={{0,4},{1,3},{2,6},{3,1},{4,0},{5,7},{6,2},{7,5},{8,12},{9,11},{10,... | collective-permute-start | bytes 344072 | tf_op jit(solution)/shard_map/ppermute | solution.py:117
  57.3 14.8 %collective-permute-start.8 = (bf16[64,1792]{1,0:T(8,128)(2,1)S(1)}, bf16[64,1792]{1,0:T(8,128)(2,1)S(1)}, u32[]{:S(2)}, u32[]{:S(2)}) collective-permute-start(bf16[64,1792]{1,0:T(8,128)(2,1)S(1)} %pad_maximum_fusion.6), channel_id=1, source_target_pairs={{0,8},{1,17},{2,10},{3,19},{4,12},{5,21},{6,14},{7,23},{8,0},{9,25... | collective-permute-start | bytes 688136 | tf_op jit(solution)/shard_map/ppermute | solution.py:117
  61.9 8.5 %collective-permute-start.12 = (bf16[64,1792]{1,0:T(8,128)(2,1)S(1)}, bf16[64,1792]{1,0:T(8,128)(2,1)S(1)}, u32[]{:S(2)}, u32[]{:S(2)}) collective-permute-start(bf16[64,1792]{1,0:T(8,128)(2,1)S(1)} %pad_maximum_fusion.7), channel_id=1, source_target_pairs={{0,8},{1,17},{2,10},{3,19},{4,12},{5,21},{6,14},{7,23},{8,0},{9,25... | collective-permute-start | bytes 688136 | tf_op jit(solution)/shard_map/ppermute | solution.py:117
  70.5 8.5 %collective-permute-start.13 = (bf16[128,1792]{1,0:T(8,128)(2,1)S(1)}, bf16[128,1792]{1,0:T(8,128)(2,1)S(1)}, u32[]{:S(2)}, u32[]{:S(2)}) collective-permute-start(bf16[128,1792]{1,0:T(8,128)(2,1)S(1)} %pad_maximum_fusion.2), channel_id=1, source_target_pairs={{0,16},{1,9},{2,18},{3,11},{4,20},{5,13},{6,22},{7,15},{8,24},{9,1... | collective-permute-start | bytes 1376264 | tf_op jit(solution)/shard_map/ppermute | solution.py:117
  72.1 11.8 %collective-permute-start.9 = (bf16[128,1792]{1,0:T(8,128)(2,1)S(1)}, bf16[128,1792]{1,0:T(8,128)(2,1)S(1)}, u32[]{:S(2)}, u32[]{:S(2)}) collective-permute-start(bf16[128,1792]{1,0:T(8,128)(2,1)S(1)} %pad_maximum_fusion.1), channel_id=1, source_target_pairs={{0,16},{1,9},{2,18},{3,11},{4,20},{5,13},{6,22},{7,15},{8,24},{9,1... | collective-permute-start | bytes 1376264 | tf_op jit(solution)/shard_map/ppermute | solution.py:117
  79.1 5.7 %collective-permute-start.15 = (bf16[256,1792]{1,0:T(8,128)(2,1)S(1)}, bf16[256,1792]{1,0:T(8,128)(2,1)S(1)}, u32[]{:S(2)}, u32[]{:S(2)}) collective-permute-start(bf16[256,1792]{1,0:T(8,128)(2,1)S(1)} %constant_dynamic-update-slice_fusion.5.rest_8_), channel_id=1, source_target_pairs={{0,1},{1,0},{2,3},{3,2},{4,5},{5,4},{6,7},{7,6},{8,9},{9,8},{10,11... | collective-permute-start | bytes 2752520 | tf_op jit(solution)/shard_map/ppermute | solution.py:108
  93.1 8.7 %collective-permute-start.17 = (bf16[128,1792]{1,0:T(8,128)(2,1)S(1)}, bf16[128,1792]{1,0:T(8,128)(2,1)S(1)}, u32[]{:S(2)}, u32[]{:S(2)}) collective-permute-start(bf16[128,1792]{1,0:T(8,128)(2,1)S(1)} %slice.651), channel_id=1, source_target_pairs={{0,16},{1,9},{2,18},{3,11},{4,20},{5,13},{6,22},{7,15},{8,24},{9,1... | collective-permute-start | bytes 1376264 | tf_op jit(solution)/shard_map/ppermute | solution.py:117
  95.6 13.7 %collective-permute-start.27 = (bf16[128,1792]{1,0:T(8,128)(2,1)S(1)}, bf16[128,1792]{1,0:T(8,128)(2,1)S(1)}, u32[]{:S(2)}, u32[]{:S(2)}) collective-permute-start(bf16[128,1792]{1,0:T(8,128)(2,1)S(1)} %slice.650), channel_id=1, source_target_pairs={{0,16},{1,9},{2,18},{3,11},{4,20},{5,13},{6,22},{7,15},{8,24},{9,1... | collective-permute-start | bytes 1376264 | tf_op jit(solution)/shard_map/ppermute | solution.py:117
  102.0 9.0 %collective-permute-start.18 = (bf16[64,1792]{1,0:T(8,128)(2,1)S(1)}, bf16[64,1792]{1,0:T(8,128)(2,1)S(1)}, u32[]{:S(2)}, u32[]{:S(2)}) collective-permute-start(bf16[64,1792]{1,0:T(8,128)(2,1)S(1)} %slice.653), channel_id=1, source_target_pairs={{0,8},{1,17},{2,10},{3,19},{4,12},{5,21},{6,14},{7,23},{8,0},{9,25... | collective-permute-start | bytes 688136 | tf_op jit(solution)/shard_map/ppermute | solution.py:117
  109.4 6.1 %collective-permute-start.28 = (bf16[64,1792]{1,0:T(8,128)(2,1)S(1)}, bf16[64,1792]{1,0:T(8,128)(2,1)S(1)}, u32[]{:S(2)}, u32[]{:S(2)}) collective-permute-start(bf16[64,1792]{1,0:T(8,128)(2,1)S(1)} %slice.652), channel_id=1, source_target_pairs={{0,8},{1,17},{2,10},{3,19},{4,12},{5,21},{6,14},{7,23},{8,0},{9,25... | collective-permute-start | bytes 688136 | tf_op jit(solution)/shard_map/ppermute | solution.py:117
  111.0 8.1 %collective-permute-start.19 = (bf16[32,1792]{1,0:T(8,128)(2,1)S(1)}, bf16[32,1792]{1,0:T(8,128)(2,1)S(1)}, u32[]{:S(2)}, u32[]{:S(2)}) collective-permute-start(bf16[32,1792]{1,0:T(8,128)(2,1)S(1)} %slice.657), channel_id=1, source_target_pairs={{0,4},{1,3},{2,6},{3,1},{4,0},{5,7},{6,2},{7,5},{8,12},{9,11},{10,... | collective-permute-start | bytes 344072 | tf_op jit(solution)/shard_map/ppermute | solution.py:117
  115.6 7.6 %collective-permute-start.29 = (bf16[32,1792]{1,0:T(8,128)(2,1)S(1)}, bf16[32,1792]{1,0:T(8,128)(2,1)S(1)}, u32[]{:S(2)}, u32[]{:S(2)}) collective-permute-start(bf16[32,1792]{1,0:T(8,128)(2,1)S(1)} %slice.656), channel_id=1, source_target_pairs={{0,4},{1,3},{2,6},{3,1},{4,0},{5,7},{6,2},{7,5},{8,12},{9,11},{10,... | collective-permute-start | bytes 344072 | tf_op jit(solution)/shard_map/ppermute | solution.py:117
  132.3 8.3 %collective-permute-start.22 = (bf16[32,1792]{1,0:T(8,128)(2,1)S(1)}, bf16[32,1792]{1,0:T(8,128)(2,1)S(1)}, u32[]{:S(2)}, u32[]{:S(2)}) collective-permute-start(bf16[32,1792]{1,0:T(8,128)(2,1)S(1)} %pad_maximum_fusion.12), channel_id=1, source_target_pairs={{0,4},{1,3},{2,6},{3,1},{4,0},{5,7},{6,2},{7,5},{8,12},{9,11},{10,... | collective-permute-start | bytes 344072 | tf_op jit(solution)/shard_map/ppermute | solution.py:117
  133.4 9.9 %collective-permute-start.32 = (bf16[32,1920]{1,0:T(8,128)(2,1)S(1)}, bf16[32,1920]{1,0:T(8,128)(2,1)S(1)}, u32[]{:S(2)}, u32[]{:S(2)}) collective-permute-start(bf16[32,1920]{1,0:T(8,128)(2,1)S(1)} %pad_maximum_fusion.9), channel_id=1, source_target_pairs={{0,4},{1,3},{2,6},{3,1},{4,0},{5,7},{6,2},{7,5},{8,12},{9,11},{10,... | collective-permute-start | bytes 368648 | tf_op jit(solution)/shard_map/ppermute | solution.py:117
  140.6 9.2 %collective-permute-start.23 = (bf16[64,1792]{1,0:T(8,128)(2,1)S(1)}, bf16[64,1792]{1,0:T(8,128)(2,1)S(1)}, u32[]{:S(2)}, u32[]{:S(2)}) collective-permute-start(bf16[64,1792]{1,0:T(8,128)(2,1)S(1)} %pad_maximum_fusion.8), channel_id=1, source_target_pairs={{0,8},{1,17},{2,10},{3,19},{4,12},{5,21},{6,14},{7,23},{8,0},{9,25... | collective-permute-start | bytes 688136 | tf_op jit(solution)/shard_map/ppermute | solution.py:117
  143.3 10.9 %collective-permute-start.33 = (bf16[64,1920]{1,0:T(8,128)(2,1)S(1)}, bf16[64,1920]{1,0:T(8,128)(2,1)S(1)}, u32[]{:S(2)}, u32[]{:S(2)}) collective-permute-start(bf16[64,1920]{1,0:T(8,128)(2,1)S(1)} %pad_maximum_fusion.4), channel_id=1, source_target_pairs={{0,8},{1,17},{2,10},{3,19},{4,12},{5,21},{6,14},{7,23},{8,0},{9,25... | collective-permute-start | bytes 737288 | tf_op jit(solution)/shard_map/ppermute | solution.py:117
  149.8 8.5 %collective-permute-start.24 = (bf16[128,1792]{1,0:T(8,128)(2,1)S(1)}, bf16[128,1792]{1,0:T(8,128)(2,1)S(1)}, u32[]{:S(2)}, u32[]{:S(2)}) collective-permute-start(bf16[128,1792]{1,0:T(8,128)(2,1)S(1)} %pad_maximum_fusion.3), channel_id=1, source_target_pairs={{0,16},{1,9},{2,18},{3,11},{4,20},{5,13},{6,22},{7,15},{8,24},{9,1... | collective-permute-start | bytes 1376264 | tf_op jit(solution)/shard_map/ppermute | solution.py:117
  154.3 9.3 %collective-permute-start.34 = (bf16[128,1920]{1,0:T(8,128)(2,1)S(1)}, bf16[128,1920]{1,0:T(8,128)(2,1)S(1)}, u32[]{:S(2)}, u32[]{:S(2)}) collective-permute-start(bf16[128,1920]{1,0:T(8,128)(2,1)S(1)} %pad_maximum_fusion), channel_id=1, source_target_pairs={{0,16},{1,9},{2,18},{3,11},{4,20},{5,13},{6,22},{7,15},{8,24},{9,1... | collective-permute-start | bytes 1474568 | tf_op jit(solution)/shard_map/ppermute | solution.py:117
  158.3 6.0 %collective-permute-start.25 = (bf16[256,1792]{1,0:T(8,128)(2,1)S(1)}, bf16[256,1792]{1,0:T(8,128)(2,1)S(1)}, u32[]{:S(2)}, u32[]{:S(2)}) collective-permute-start(bf16[256,1792]{1,0:T(8,128)(2,1)S(1)} %constant_dynamic-update-slice_fusion.10.rest_10_), channel_id=1, source_target_pairs={{0,1},{1,0},{2,3},{3,2},{4,5},{5,4},{6,7},{7,6},{8,9},{9,8},{10,11... | collective-permute-start | bytes 2752520 | tf_op jit(solution)/shard_map/ppermute | solution.py:108
  (27 other events, 161.0 us)
where the time goes:
time: 178 us
  waiting for transfers between devices  83.3 us (47%)
  starting transfers between devices  39.7 us (22%)
  matrix products  18.3 us (10%)
  blocking collectives  17.9 us (10%)
  Pallas kernels  11.4 us (6%)
  local copies, waits for them, and re-layouts  4.27 us (2%)
  other arithmetic  1.99 us (1%)
    ppermute x28, waiting for transfers between devices, exchange(): return lax.ppermute(value, both, pairs)  79.3 us
    ppermute x28, starting transfers between devices, exchange(): return lax.ppermute(value, both, pairs)  38.1 us
    dot_general x15, matrix products, dot(): lax.dot_general(left, right, (((left_dim,), (right_dim,)), ((), ())), pre...  18.3 us
    all_gather x1, blocking collectives, whole_step(): full_rows = lax.all_gather(residual_in, 'mp', axis=1, tiled=True)  17.9 us
    pallas_call x1, Pallas kernels, whole_step(): pl.pallas_call(functools.partial(finish, len(err_all), float(tokens * wid...  11.4 us
    ppermute x8, waiting for transfers between devices, other_core(): lax.ppermute(value, both, [(d * n_mp + m, d * n_mp + (m ^ 1)) for d, m in...  4.05 us
    unnamed x42, local copies, waits for them, and re-layouts  3.72 us
  transfers between devices with their start and end apart: 36, of which 26 were waited for; matrix products, arithmetic and copies ran while one was open for 4% of the time, Pallas kernels for 0%

commit v1 on v0

--- a/solution.py
+++ b/solution.py
@@ -24,14 +24,42 @@
     )
 
 
-def finish(n_parts, entries, thr_ref, w_dec_ref, *rest):
-    pairs = [rest[2 * i : 2 * i + 2] for i in range(3 + 2 * n_parts)]
-    pre_refs, partial_refs, feat_refs = pairs[:3]
-    layer_refs, err_refs = pairs[3 : 3 + n_parts], pairs[3 + n_parts :]
-    wenc_ref, wdec_ref, gthr_ref, gbenc_ref, gbdec_ref, loss_ref, buffer, sems = rest[-8:]
-    span = err_refs[0][0].shape[1]
+def turn_body(near_ref, far_ref, turned_ref):
+    count = near_ref.shape[0]
+    turned_ref[:, :count] = near_ref[...].T
+    turned_ref[:, count:] = far_ref[...].T
+
+
+def row_body(source_ref, row_ref):
+    row_ref[...] = source_ref[...]
+
+
+def row_of(values):
+    vmem = pl.BlockSpec(memory_space=pltpu.VMEM)
+    return pl.pallas_call(
+        row_body,
+        out_shape=jax.ShapeDtypeStruct((1, values.shape[0]), values.dtype),
+        in_specs=[vmem],
+        out_specs=vmem,
+        name="row",
+    )(values[None, :])
+
+
+def side_by_side(pair):
+    near, far = pair
+    vmem = pl.BlockSpec(memory_space=pltpu.VMEM)
+    return pl.pallas_call(
+        turn_body,
+        out_shape=jax.ShapeDtypeStruct((near.shape[1], 2 * near.shape[0]), near.dtype),
+        in_specs=[vmem] * 2,
+        out_specs=vmem,
+        compiler_params=pltpu.CompilerParams(vmem_limit_bytes=40 * 2**20),
+        name="turn",
+    )(near, far)
+
+
+def sender(buffer, sems):
     n_slots = buffer.shape[0]
-    step = buffer.shape[1]
     copies = []
 
     def send(value, target):
@@ -46,25 +74,51 @@
         copy.start()
         copies.append(copy)
 
-    def grad_wdec(i):
-        for low in range(0, span, step):
-            size = min(step, span - low)
-            value = sum(
-                dot(feat[...], err[:, low : low + size], 0, 0)
-                for feat, err in zip(feat_refs, err_refs[i])
-            )
-            send(value, wdec_ref.at[:, pl.ds(i * span + low, size)])
-            ones = jnp.ones((8, err_refs[i][0].shape[0]), bf16)
-            gbdec_ref[:, i * span + low : i * span + low + size] = sum(
-                dot(ones, err[:, low : low + size], 1, 0)[:1] for err in err_refs[i]
-            )
-
-    for i in range(n_parts - 1):
-        grad_wdec(i)
-
-    weight = w_dec_ref[:, (n_parts - 1) * span :]
+    def drain():
+        for copy in copies[-n_slots:]:
+            copy.wait()
+
+    return send, drain
+
+
+def grad_wdec(send, feat_ref, errs, wdec_ref, gbdec_ref, base, span, step):
+    near = errs[0].shape[0]
+    ones = jnp.ones((8, near), bf16)
+    for low in range(0, span, step):
+        cols = slice(low, min(low + step, span))
+        value = sum(
+            dot(feat_ref[:, side * near : (side + 1) * near], err[:, cols], 1, 0)
+            for side, err in enumerate(errs)
+        )
+        send(value, wdec_ref.at[:, pl.ds(base + low, cols.stop - low)])
+        gbdec_ref[:, cols] = sum(dot(ones, err[:, cols], 1, 0)[:1] for err in errs)
+
+
+def early_body(
+    step, feat_ref, w_dec_ref, near_ref, far_ref, wdec_ref, gbdec_ref, *rest
+):
+    near_out, far_out, buffer, sems = rest
+    span = near_ref.shape[1]
+    send, drain = sender(buffer, sems)
+    grad_wdec(
+        send, feat_ref, (near_ref, far_ref), wdec_ref, gbdec_ref, 0, span, step
+    )
+    weight = w_dec_ref[:, :span]
+    near_out[...] = dot(near_ref[...], weight, 1, 1)
+    far_out[...] = dot(far_ref[...], weight, 1, 1)
+    drain()
+
+
+def finish_body(
+    step, entries, _, thr_ref, w_dec_ref, feat_ref, first_ref, second_ref, *rest
+):
+    pre_refs, partial_refs, err_refs = rest[:2], rest[2:4], rest[4:6]
+    wenc_ref, wdec_ref, gthr_ref, gbenc_ref, gbdec_ref, loss_ref, buffer, sems = rest[6:]
+    span = first_ref.shape[0]
+    send, drain = sender(buffer, sems)
+    weight = w_dec_ref[:, span:]
     grads, sums_thr, sums_benc = [], 0.0, 0.0
-    for pre_ref, partial_ref, err_ref in zip(pre_refs, partial_refs, err_refs[-1]):
+    for pre_ref, partial_ref, err_ref in zip(pre_refs, partial_refs, err_refs):
         grad_feat = partial_ref[...] + dot(err_ref[:, :span], weight, 1, 1)
         pre = pre_ref[...]
         soft = jax.nn.sigmoid((pre - thr_ref[...]) / gate_band)
@@ -76,22 +130,19 @@
         grads.append(grad.astype(bf16))
     shares = sum(
         jnp.sum(err_ref[:, span:].astype(f32), axis=0, keepdims=True)
-        for err_ref in err_refs[-1]
+        for err_ref in err_refs
     )
     loss_ref[0, 0] = jnp.sum(shares) / entries
     gthr_ref[...] = sums_thr
     gbenc_ref[...] = sums_benc
-    for i, layers in enumerate(layer_refs):
+    grads = jnp.concatenate(grads, axis=0)
+    for i, layer_ref in enumerate((first_ref, second_ref)):
         for low in range(0, span, step):
             size = min(step, span - low)
-            value = sum(
-                dot(layer[:, low : low + size], grad, 0, 0)
-                for layer, grad in zip(layers, grads)
-            )
+            value = dot(layer_ref[low : low + size, :], grads, 1, 0)
             send(value, wenc_ref.at[pl.ds(i * span + low, size), :])
-    grad_wdec(n_parts - 1)
-    for copy in copies[-n_slots:]:
-        copy.wait()
+    grad_wdec(send, feat_ref, err_refs, wdec_ref, gbdec_ref, span, span, step)
+    drain()
 
 
 def program(n_dp, n_mp):
@@ -186,16 +237,12 @@
             layer_out.append((near, other_core(near)))
         sides = range(2)
 
-        def over(parts, weight, dim, side, leave=0):
-            return sum(
-                dot(part[side], weight(cols), 1, dim)
-                for part, cols in list(zip(parts, columns(len(parts))))[: len(parts) - leave]
-            )
-
-        pre_act = [
-            over(layer_out, lambda cols: w_enc[cols, :], 0, side) + b_enc[None, :]
-            for side in sides
-        ]
+        cols = columns(2)
+        pre_act = []
+        for side in sides:
+            first = dot(layer_out[0][side], w_enc[cols[0], :], 1, 0) + b_enc[None, :]
+            first = lax.optimization_barrier(first)
+            pre_act.append(first + dot(layer_out[1][side], w_enc[cols[1], :], 1, 0))
         soft = [jax.nn.sigmoid((pre - threshold[None, :]) / gate_band) for pre in pre_act]
         feat = [(pre * open_).astype(bf16) for pre, open_ in zip(pre_act, soft)]
         lanes = 128
@@ -234,35 +281,60 @@
 
         vmem = pl.BlockSpec(memory_space=pltpu.VMEM)
         hbm = pl.BlockSpec(memory_space=pl.ANY)
-        features = w_enc.shape[1]
-        pairs = [pre_act]
-        pairs.append(
-            [over(err_all, lambda cols: w_dec[:, cols], 1, side, 1) for side in sides]
-        )
-        pairs += [feat] + layer_out + err_all
-        operands = [threshold[None, :], w_dec] + [part for pair in pairs for part in pair]
-        n_slots = 4
-        grad_wenc, grad_wdec, grad_thresh, grad_benc, grad_bdec, shares = pl.pallas_call(
-            functools.partial(finish, len(err_all), float(tokens * width)),
+        features, span, step = w_enc.shape[1], width // 2, 512
+        turned = []
+        for pair in layer_out:
+            turned.append(side_by_side(pair))
+        threshold_row = row_of(threshold)
+        feat_turned = side_by_side(feat)
+        scratch = [
+            pltpu.VMEM((4, max(step, features), max(step, features)), bf16),
+            pltpu.SemaphoreType.DMA((4,)),
+        ]
+        params = pltpu.CompilerParams(vmem_limit_bytes=40 * 2**20)
+        rows = pre_act[0].shape[0]
+        grad_wdec, bdec_first, *partial = pl.pallas_call(
+            functools.partial(early_body, step),
+            out_shape=(
+                jax.ShapeDtypeStruct((features, width), bf16),
+                jax.ShapeDtypeStruct((1, span), f32),
+                jax.ShapeDtypeStruct((rows, features), f32),
+                jax.ShapeDtypeStruct((rows, features), f32),
+            ),
+            in_specs=[vmem] * 4,
+            out_specs=(hbm, vmem, vmem, vmem),
+            scratch_shapes=scratch,
+            compiler_params=params,
+            name="early",
+        )(feat_turned, w_dec, *err_all[0])
+        grad_wenc, grad_wdec, grad_thresh, grad_benc, bdec_second, loss = pl.pallas_call(
+            functools.partial(finish_body, step, float(tokens * width)),
             out_shape=(
                 jax.ShapeDtypeStruct((width, features), bf16),
                 jax.ShapeDtypeStruct((features, width), bf16),
                 jax.ShapeDtypeStruct((1, features), f32),
                 jax.ShapeDtypeStruct((1, features), f32),
-                jax.ShapeDtypeStruct((1, width), f32),
+                jax.ShapeDtypeStruct((1, span), f32),
                 jax.ShapeDtypeStruct((1, 1), f32),
             ),
-            in_specs=[vmem] * len(operands),
+            in_specs=[hbm] + [vmem] * 11,
             out_specs=(hbm, hbm, vmem, vmem, vmem, pl.BlockSpec(memory_space=pltpu.SMEM)),
-            scratch_shapes=[
-                pltpu.VMEM((n_slots, 512, 512), bf16),
-                pltpu.SemaphoreType.DMA((n_slots,)),
-            ],
-            compiler_params=pltpu.CompilerParams(vmem_limit_bytes=40 * 2**20),
+            input_output_aliases={0: 1},
+            scratch_shapes=scratch,
+            compiler_params=params,
             name="finish",
-        )(*operands)
-        grad_thresh, grad_benc, grad_bdec = grad_thresh[0], grad_benc[0], grad_bdec[0]
-        loss_value = shares[0, 0]
+        )(
+            grad_wdec,
+            threshold_row,
+            w_dec,
+            feat_turned,
+            *turned,
+            *pre_act,
+            *partial,
+            *err_all[1],
+        )
+        grad_bdec = jnp.concatenate([bdec_first, bdec_second], axis=1)[0]
+        grad_thresh, grad_benc, loss_value = grad_thresh[0], grad_benc[0], loss[0, 0]
         return (loss_value, grad_wenc, grad_wdec, grad_benc, grad_thresh, grad_bdec)
 
     return whole_step

time: 178 us -> 193 us (1.084)
  local copies, waits for them, and re-layouts: 4.27 us -> 13.2 us
  waiting for transfers between devices: 83.3 us -> 89.1 us
  starting transfers between devices: 39.7 us -> 35.5 us
  Pallas kernels: 11.4 us -> 15.2 us
    unnamed x42 -> x58, local copies, waits for them, and re-layouts: 3.72 us -> 11.9 us
    ppermute x28, waiting for transfers between devices: 79.3 us -> 87.4 us  [exchange(): return lax.ppermute(value, both, pairs)]
    ppermute x28, starting transfers between devices: 38.1 us -> 34 us  [exchange(): return lax.ppermute(value, both, pairs)]
    pallas_call x1 -> x6, Pallas kernels: 11.4 us -> 15.2 us  [the longest x1 8.43 us: whole_step(): pl.pallas_call(functools.partial(finish_body, step, float(tokens * width)...]
    ppermute x8, waiting for transfers between devices: 4.05 us -> 1.72 us  [other_core(): lax.ppermute(value, both, [(d * n_mp + m, d * n_mp + (m ^ 1)) for d, m in...]
    dot_general x15 -> x13, matrix products: 18.3 us -> 17 us  [dot(): lax.dot_general(left, right, (((left_dim,), (right_dim,)), ((), ())), pre...]
  transfers between devices with their start and end apart: 36 -> 36, of which waited for: 26 -> 24; matrix products, arithmetic and copies ran while one was open for 4% -> 5% of each run, Pallas kernels for 0% -> 4%
where the time goes in v1:
time: 193 us
  waiting for transfers between devices  89.1 us (46%)
  starting transfers between devices  35.5 us (18%)
  blocking collectives  17.9 us (9%)
  matrix products  17 us (9%)
  Pallas kernels  15.2 us (8%)
  local copies, waits for them, and re-layouts  13.2 us (7%)
  other arithmetic  3.24 us (2%)
    ppermute x28, waiting for transfers between devices, exchange(): return lax.ppermute(value, both, pairs)  87.4 us
    ppermute x28, starting transfers between devices, exchange(): return lax.ppermute(value, both, pairs)  34 us
    all_gather x1, blocking collectives, whole_step(): full_rows = lax.all_gather(residual_in, 'mp', axis=1, tiled=True)  17.9 us
    dot_general x13, matrix products, dot(): lax.dot_general(left, right, (((left_dim,), (right_dim,)), ((), ())), pre...  17 us
    unnamed x58, local copies, waits for them, and re-layouts  11.9 us
    pallas_call x1, Pallas kernels, whole_step(): pl.pallas_call(functools.partial(finish_body, step, float(tokens * width)...  8.43 us
    pallas_call x1, Pallas kernels, whole_step(): pl.pallas_call(functools.partial(early_body, step), out_shape=(jax.ShapeD...  4.32 us
  transfers between devices with their start and end apart: 36, of which 24 were waited for; matrix products, arithmetic and copies ran while one was open for 5% of the time, Pallas kernels for 4%

profile of v1, /device:TPU:0, one launch (start us, length us, event | category | flops | bytes accessed | tf_op | source)
XLA Modules:
  0.0 192.6 jit_solution(8487566798263493140)
XLA Ops:
  0.9 17.9 %all_gather.3 = bf16[128,3584]{0,1:T(8,128)(2,1)S(1)} all-gather(bf16[128,448]{0,1:T(8,128)(2,1)} %param.11), channel_id=1, replica_groups=mesh['dp'=4,'mp'=8] {'mp'}, dimensions={1}, use_global_device_ids=true | all-gather | bytes 1032192 | tf_op jit(solution)/shard_map/all_gather | solution.py:196
  19.5 6.9 %fusion.61 = f32[128,1792]{1,0:T(8,128)S(1)} fusion(bf16[3584,1792]{1,0:T(8,128)(2,1)} %param.14, f32[128,3584]{1,0:T(8,128)S(1)} %get-tuple-element.50, f32[3584]{0:T(1024)S(1)} %copy-done.9, f32[128]{0:T(128)S(1)} %add_rsqrt_fusion.1), kind=kOutput, calls=%fused_computation.184 | convolution fusion | flops 1645543424 | bytes 15612416 | tf_op jit(solution)/shard_map/dot_general | solution.py:22
  27.3 2.2 %fusion.5 = bf16[128,1792]{1,0:T(8,128)(2,1)S(1)} fusion(bf16[3584,1792]{1,0:T(8,128)(2,1)S(1)} %bitcast.26, f32[128,1792]{1,0:T(8,128)S(1)} %fusion.61, f32[128,3584]{1,0:T(8,128)S(1)} %get-tuple-element.50, f32[3584]{0:T(1024)S(1)} %copy-done.9, f32[128]{0:T(128)S(1)} %add_rsqrt_fusion.1), kind=kOutput, calls=%fused_computation.9 | convolution fusion | flops 1647837184 | bytes 16071168 | tf_op jit(solution)/shard_map/dot_general | solution.py:22
  36.9 2.7 %collective-permute-done.4 = bf16[32,1792]{1,0:T(8,128)(2,1)S(1)} collective-permute-done((bf16[32,1792]{1,0:T(8,128)(2,1)S(1)}, bf16[32,1792]{1,0:T(8,128)(2,1)S(1)}, u32[]{:S(2)}, u32[]{:S(2)}) %collective-permute-start.4) | collective-permute-done | bytes 114720 | tf_op jit(solution)/shard_map/ppermute | solution.py:168
  39.7 3.0 %collective-permute-start.5 = (bf16[16,1792]{1,0:T(8,128)(2,1)S(1)}, bf16[16,1792]{1,0:T(8,128)(2,1)S(1)}, u32[]{:S(2)}, u32[]{:S(2)}) collective-permute-start(bf16[16,1792]{1,0:T(8,128)(2,1)S(1)} %slice.652), channel_id=1, source_target_pairs={{0,2},{1,5},{2,0},{3,7},{4,6},{5,1},{6,4},{7,3},{8,10},{9,13},{10,... | collective-permute-start | bytes 172040 | tf_op jit(solution)/shard_map/ppermute | solution.py:168
  51.5 2.9 %collective-permute-start.11 = (bf16[32,1792]{1,0:T(8,128)(2,1)S(1)}, bf16[32,1792]{1,0:T(8,128)(2,1)S(1)}, u32[]{:S(2)}, u32[]{:S(2)}) collective-permute-start(bf16[32,1792]{1,0:T(8,128)(2,1)S(1)} %pad_maximum_fusion.11), channel_id=1, source_target_pairs={{0,4},{1,3},{2,6},{3,1},{4,0},{5,7},{6,2},{7,5},{8,12},{9,11},{10,... | collective-permute-start | bytes 344072 | tf_op jit(solution)/shard_map/ppermute | solution.py:168
  54.4 2.4 %collective-permute-start.7 = (bf16[32,1792]{1,0:T(8,128)(2,1)S(1)}, bf16[32,1792]{1,0:T(8,128)(2,1)S(1)}, u32[]{:S(2)}, u32[]{:S(2)}) collective-permute-start(bf16[32,1792]{1,0:T(8,128)(2,1)S(1)} %pad_maximum_fusion.10), channel_id=1, source_target_pairs={{0,4},{1,3},{2,6},{3,1},{4,0},{5,7},{6,2},{7,5},{8,12},{9,11},{10,... | collective-permute-start | bytes 344072 | tf_op jit(solution)/shard_map/ppermute | solution.py:168
  58.9 3.0 %collective-permute-done.7 = bf16[32,1792]{1,0:T(8,128)(2,1)S(1)} collective-permute-done((bf16[32,1792]{1,0:T(8,128)(2,1)S(1)}, bf16[32,1792]{1,0:T(8,128)(2,1)S(1)}, u32[]{:S(2)}, u32[]{:S(2)}) %collective-permute-start.7) | collective-permute-done | bytes 114720 | tf_op jit(solution)/shard_map/ppermute | solution.py:168
  63.5 7.0 %collective-permute-done.8 = bf16[64,1792]{1,0:T(8,128)(2,1)S(1)} collective-permute-done((bf16[64,1792]{1,0:T(8,128)(2,1)S(1)}, bf16[64,1792]{1,0:T(8,128)(2,1)S(1)}, u32[]{:S(2)}, u32[]{:S(2)}) %collective-permute-start.8) | collective-permute-done | bytes 229408 | tf_op jit(solution)/shard_map/ppermute | solution.py:168
  72.7 6.3 %collective-permute-done.9 = bf16[128,1792]{1,0:T(8,128)(2,1)S(1)} collective-permute-done((bf16[128,1792]{1,0:T(8,128)(2,1)S(1)}, bf16[128,1792]{1,0:T(8,128)(2,1)S(1)}, u32[]{:S(2)}, u32[]{:S(2)}) %collective-permute-start.9) | collective-permute-done | bytes 458784 | tf_op jit(solution)/shard_map/ppermute | solution.py:168
  79.2 4.8 %collective-permute-done.13 = bf16[128,1792]{1,0:T(8,128)(2,1)S(1)} collective-permute-done((bf16[128,1792]{1,0:T(8,128)(2,1)S(1)}, bf16[128,1792]{1,0:T(8,128)(2,1)S(1)}, u32[]{:S(2)}, u32[]{:S(2)}) %collective-permute-start.13) | collective-permute-done | bytes 458784 | tf_op jit(solution)/shard_map/ppermute | solution.py:168
  97.2 5.6 %collective-permute-done.17 = bf16[128,1792]{1,0:T(8,128)(2,1)S(1)} collective-permute-done((bf16[128,1792]{1,0:T(8,128)(2,1)S(1)}, bf16[128,1792]{1,0:T(8,128)(2,1)S(1)}, u32[]{:S(2)}, u32[]{:S(2)}) %collective-permute-start.17) | collective-permute-done | bytes 458784 | tf_op jit(solution)/shard_map/ppermute | solution.py:168
  104.5 5.7 %collective-permute-done.27 = bf16[128,1792]{1,0:T(8,128)(2,1)S(1)} collective-permute-done((bf16[128,1792]{1,0:T(8,128)(2,1)S(1)}, bf16[128,1792]{1,0:T(8,128)(2,1)S(1)}, u32[]{:S(2)}, u32[]{:S(2)}) %collective-permute-start.27) | collective-permute-done | bytes 458784 | tf_op jit(solution)/shard_map/ppermute | solution.py:168
  112.0 4.4 %collective-permute-done.28 = bf16[64,1792]{1,0:T(8,128)(2,1)S(1)} collective-permute-done((bf16[64,1792]{1,0:T(8,128)(2,1)S(1)}, bf16[64,1792]{1,0:T(8,128)(2,1)S(1)}, u32[]{:S(2)}, u32[]{:S(2)}) %collective-permute-start.28) | collective-permute-done | bytes 229408 | tf_op jit(solution)/shard_map/ppermute | solution.py:168
  116.6 3.3 %collective-permute-done.19 = bf16[32,1792]{1,0:T(8,128)(2,1)S(1)} collective-permute-done((bf16[32,1792]{1,0:T(8,128)(2,1)S(1)}, bf16[32,1792]{1,0:T(8,128)(2,1)S(1)}, u32[]{:S(2)}, u32[]{:S(2)}) %collective-permute-start.19) | collective-permute-done | bytes 114720 | tf_op jit(solution)/shard_map/ppermute | solution.py:168
  120.3 4.5 %collective-permute-done.29 = bf16[32,1792]{1,0:T(8,128)(2,1)S(1)} collective-permute-done((bf16[32,1792]{1,0:T(8,128)(2,1)S(1)}, bf16[32,1792]{1,0:T(8,128)(2,1)S(1)}, u32[]{:S(2)}, u32[]{:S(2)}) %collective-permute-start.29) | collective-permute-done | bytes 114720 | tf_op jit(solution)/shard_map/ppermute | solution.py:168
  125.3 5.0 %collective-permute-done.30 = bf16[16,1792]{1,0:T(8,128)(2,1)S(1)} collective-permute-done((bf16[16,1792]{1,0:T(8,128)(2,1)S(1)}, bf16[16,1792]{1,0:T(8,128)(2,1)S(1)}, u32[]{:S(2)}, u32[]{:S(2)}) %collective-permute-start.30) | collective-permute-done | bytes 57376 | tf_op jit(solution)/shard_map/ppermute | solution.py:168
  136.1 3.0 %collective-permute-start.32 = (bf16[32,1920]{1,0:T(8,128)(2,1)S(1)}, bf16[32,1920]{1,0:T(8,128)(2,1)S(1)}, u32[]{:S(2)}, u32[]{:S(2)}) collective-permute-start(bf16[32,1920]{1,0:T(8,128)(2,1)S(1)} %pad_maximum_fusion.9), channel_id=1, source_target_pairs={{0,4},{1,3},{2,6},{3,1},{4,0},{5,7},{6,2},{7,5},{8,12},{9,11},{10,... | collective-permute-start | bytes 368648 | tf_op jit(solution)/shard_map/ppermute | solution.py:168
  139.1 4.6 %collective-permute-done.22 = bf16[32,1792]{1,0:T(8,128)(2,1)S(1)} collective-permute-done((bf16[32,1792]{1,0:T(8,128)(2,1)S(1)}, bf16[32,1792]{1,0:T(8,128)(2,1)S(1)}, u32[]{:S(2)}, u32[]{:S(2)}) %collective-permute-start.22) | collective-permute-done | bytes 114720 | tf_op jit(solution)/shard_map/ppermute | solution.py:168
  146.5 11.0 %collective-permute-done.33 = bf16[64,1920]{1,0:T(8,128)(2,1)S(1)} collective-permute-done((bf16[64,1920]{1,0:T(8,128)(2,1)S(1)}, bf16[64,1920]{1,0:T(8,128)(2,1)S(1)}, u32[]{:S(2)}, u32[]{:S(2)}) %collective-permute-start.33) | collective-permute-done | bytes 245792 | tf_op jit(solution)/shard_map/ppermute | solution.py:168
  160.5 6.0 %collective-permute-done.34 = bf16[128,1920]{1,0:T(8,128)(2,1)S(1)} collective-permute-done((bf16[128,1920]{1,0:T(8,128)(2,1)S(1)}, bf16[128,1920]{1,0:T(8,128)(2,1)S(1)}, u32[]{:S(2)}, u32[]{:S(2)}) %collective-permute-start.34) | collective-permute-done | bytes 491552 | tf_op jit(solution)/shard_map/ppermute | solution.py:168
  166.6 4.8 %collective-permute-done.24 = bf16[128,1792]{1,0:T(8,128)(2,1)S(1)} collective-permute-done((bf16[128,1792]{1,0:T(8,128)(2,1)S(1)}, bf16[128,1792]{1,0:T(8,128)(2,1)S(1)}, u32[]{:S(2)}, u32[]{:S(2)}) %collective-permute-start.24) | collective-permute-done | bytes 458784 | tf_op jit(solution)/shard_map/ppermute | solution.py:168
  179.2 4.3 %early.1 = (bf16[512,3584]{1,0:T(8,128)(2,1)}, f32[1,1792]{1,0:T(1,128)S(1)}, f32[256,512]{1,0:T(8,128)S(1)}, f32[256,512]{1,0:T(8,128)S(1)}) custom-call(bf16[512,512]{1,0:T(8,128)(2,1)S(1)} %turn.3.feat_ref, bf16[512,3584]{1,0:T(8,128)(2,1)S(1)} %copy-done.1, bf16[256,1792]{1,0:T(8,128)(2,1)} %constant_dynamic-update-slice_fusion.10.near_ref, ...), custom_call_target="tpu_custom_call" | custom-call | tf_op jit(solution)/shard_map/early/pallas_call | solution.py:296
  183.5 8.4 %finish.1 = (bf16[3584,512]{1,0:T(8,128)(2,1)}, bf16[512,3584]{1,0:T(8,128)(2,1)}, f32[1,512]{1,0:T(1,128)}, f32[1,512]{1,0:T(1,128)}, f32[1,1792]{1,0:T(1,128)S(1)}, /*index=5*/f32[1,1]{1,0:T(1,128)}) custom-call(bf16[512,3584]{1,0:T(8,128)(2,1)} %get-tuple-element.16._, f32[1,512]{1,0:T(1,128)S(1)} %copy-done.8, ...), custom_call_target="tpu_custom_call", output_to_operand_aliasing={{1}: (0, {})} | custom-call | tf_op jit(solution)/shard_map/finish/pallas_call | solution.py:310
  (193 shorter events, 61.6 us)
Async XLA Ops:
  33.8 5.9 %collective-permute-start.4 = (bf16[32,1792]{1,0:T(8,128)(2,1)S(1)}, bf16[32,1792]{1,0:T(8,128)(2,1)S(1)}, u32[]{:S(2)}, u32[]{:S(2)}) collective-permute-start(bf16[32,1792]{1,0:T(8,128)(2,1)S(1)} %slice.648), channel_id=1, source_target_pairs={{0,4},{1,3},{2,6},{3,1},{4,0},{5,7},{6,2},{7,5},{8,12},{9,11},{10,... | collective-permute-start | bytes 344072 | tf_op jit(solution)/shard_map/ppermute | solution.py:168
  35.1 7.6 %collective-permute-start.1 = (bf16[32,1792]{1,0:T(8,128)(2,1)S(1)}, bf16[32,1792]{1,0:T(8,128)(2,1)S(1)}, u32[]{:S(2)}, u32[]{:S(2)}) collective-permute-start(bf16[32,1792]{1,0:T(8,128)(2,1)S(1)} %slice.649), channel_id=1, source_target_pairs={{0,4},{1,3},{2,6},{3,1},{4,0},{5,7},{6,2},{7,5},{8,12},{9,11},{10,... | collective-permute-start | bytes 344072 | tf_op jit(solution)/shard_map/ppermute | solution.py:168
  51.5 5.8 %collective-permute-start.11 = (bf16[32,1792]{1,0:T(8,128)(2,1)S(1)}, bf16[32,1792]{1,0:T(8,128)(2,1)S(1)}, u32[]{:S(2)}, u32[]{:S(2)}) collective-permute-start(bf16[32,1792]{1,0:T(8,128)(2,1)S(1)} %pad_maximum_fusion.11), channel_id=1, source_target_pairs={{0,4},{1,3},{2,6},{3,1},{4,0},{5,7},{6,2},{7,5},{8,12},{9,11},{10,... | collective-permute-start | bytes 344072 | tf_op jit(solution)/shard_map/ppermute | solution.py:168
  54.4 7.5 %collective-permute-start.7 = (bf16[32,1792]{1,0:T(8,128)(2,1)S(1)}, bf16[32,1792]{1,0:T(8,128)(2,1)S(1)}, u32[]{:S(2)}, u32[]{:S(2)}) collective-permute-start(bf16[32,1792]{1,0:T(8,128)(2,1)S(1)} %pad_maximum_fusion.10), channel_id=1, source_target_pairs={{0,4},{1,3},{2,6},{3,1},{4,0},{5,7},{6,2},{7,5},{8,12},{9,11},{10,... | collective-permute-start | bytes 344072 | tf_op jit(solution)/shard_map/ppermute | solution.py:168
  57.3 14.8 %collective-permute-start.12 = (bf16[64,1792]{1,0:T(8,128)(2,1)S(1)}, bf16[64,1792]{1,0:T(8,128)(2,1)S(1)}, u32[]{:S(2)}, u32[]{:S(2)}) collective-permute-start(bf16[64,1792]{1,0:T(8,128)(2,1)S(1)} %pad_maximum_fusion.7), channel_id=1, source_target_pairs={{0,8},{1,17},{2,10},{3,19},{4,12},{5,21},{6,14},{7,23},{8,0},{9,25... | collective-permute-start | bytes 688136 | tf_op jit(solution)/shard_map/ppermute | solution.py:168
  61.9 8.5 %collective-permute-start.8 = (bf16[64,1792]{1,0:T(8,128)(2,1)S(1)}, bf16[64,1792]{1,0:T(8,128)(2,1)S(1)}, u32[]{:S(2)}, u32[]{:S(2)}) collective-permute-start(bf16[64,1792]{1,0:T(8,128)(2,1)S(1)} %pad_maximum_fusion.6), channel_id=1, source_target_pairs={{0,8},{1,17},{2,10},{3,19},{4,12},{5,21},{6,14},{7,23},{8,0},{9,25... | collective-permute-start | bytes 688136 | tf_op jit(solution)/shard_map/ppermute | solution.py:168
  70.5 8.5 %collective-permute-start.9 = (bf16[128,1792]{1,0:T(8,128)(2,1)S(1)}, bf16[128,1792]{1,0:T(8,128)(2,1)S(1)}, u32[]{:S(2)}, u32[]{:S(2)}) collective-permute-start(bf16[128,1792]{1,0:T(8,128)(2,1)S(1)} %pad_maximum_fusion.1), channel_id=1, source_target_pairs={{0,16},{1,9},{2,18},{3,11},{4,20},{5,13},{6,22},{7,15},{8,24},{9,1... | collective-permute-start | bytes 1376264 | tf_op jit(solution)/shard_map/ppermute | solution.py:168
  72.1 11.8 %collective-permute-start.13 = (bf16[128,1792]{1,0:T(8,128)(2,1)S(1)}, bf16[128,1792]{1,0:T(8,128)(2,1)S(1)}, u32[]{:S(2)}, u32[]{:S(2)}) collective-permute-start(bf16[128,1792]{1,0:T(8,128)(2,1)S(1)} %pad_maximum_fusion.2), channel_id=1, source_target_pairs={{0,16},{1,9},{2,18},{3,11},{4,20},{5,13},{6,22},{7,15},{8,24},{9,1... | collective-permute-start | bytes 1376264 | tf_op jit(solution)/shard_map/ppermute | solution.py:168
  79.1 6.5 %collective-permute-start.14 = (bf16[256,1792]{1,0:T(8,128)(2,1)S(1)}, bf16[256,1792]{1,0:T(8,128)(2,1)S(1)}, u32[]{:S(2)}, u32[]{:S(2)}) collective-permute-start(bf16[256,1792]{1,0:T(8,128)(2,1)S(1)} %constant_dynamic-update-slice_fusion.near_ref), channel_id=1, source_target_pairs={{0,1},{1,0},{2,3},{3,2},{4,5},{5,4},{6,7},{7,6},{8,9},{9,8},{10,11... | collective-permute-start | bytes 2752520 | tf_op jit(solution)/shard_map/ppermute | solution.py:159
  94.3 8.5 %collective-permute-start.17 = (bf16[128,1792]{1,0:T(8,128)(2,1)S(1)}, bf16[128,1792]{1,0:T(8,128)(2,1)S(1)}, u32[]{:S(2)}, u32[]{:S(2)}) collective-permute-start(bf16[128,1792]{1,0:T(8,128)(2,1)S(1)} %slice.641), channel_id=1, source_target_pairs={{0,16},{1,9},{2,18},{3,11},{4,20},{5,13},{6,22},{7,15},{8,24},{9,1... | collective-permute-start | bytes 1376264 | tf_op jit(solution)/shard_map/ppermute | solution.py:168
  96.6 13.6 %collective-permute-start.27 = (bf16[128,1792]{1,0:T(8,128)(2,1)S(1)}, bf16[128,1792]{1,0:T(8,128)(2,1)S(1)}, u32[]{:S(2)}, u32[]{:S(2)}) collective-permute-start(bf16[128,1792]{1,0:T(8,128)(2,1)S(1)} %slice.640), channel_id=1, source_target_pairs={{0,16},{1,9},{2,18},{3,11},{4,20},{5,13},{6,22},{7,15},{8,24},{9,1... | collective-permute-start | bytes 1376264 | tf_op jit(solution)/shard_map/ppermute | solution.py:168
  103.0 9.0 %collective-permute-start.18 = (bf16[64,1792]{1,0:T(8,128)(2,1)S(1)}, bf16[64,1792]{1,0:T(8,128)(2,1)S(1)}, u32[]{:S(2)}, u32[]{:S(2)}) collective-permute-start(bf16[64,1792]{1,0:T(8,128)(2,1)S(1)} %slice.643), channel_id=1, source_target_pairs={{0,8},{1,17},{2,10},{3,19},{4,12},{5,21},{6,14},{7,23},{8,0},{9,25... | collective-permute-start | bytes 688136 | tf_op jit(solution)/shard_map/ppermute | solution.py:168
  110.3 6.1 %collective-permute-start.28 = (bf16[64,1792]{1,0:T(8,128)(2,1)S(1)}, bf16[64,1792]{1,0:T(8,128)(2,1)S(1)}, u32[]{:S(2)}, u32[]{:S(2)}) collective-permute-start(bf16[64,1792]{1,0:T(8,128)(2,1)S(1)} %slice.642), channel_id=1, source_target_pairs={{0,8},{1,17},{2,10},{3,19},{4,12},{5,21},{6,14},{7,23},{8,0},{9,25... | collective-permute-start | bytes 688136 | tf_op jit(solution)/shard_map/ppermute | solution.py:168
  112.0 7.9 %collective-permute-start.19 = (bf16[32,1792]{1,0:T(8,128)(2,1)S(1)}, bf16[32,1792]{1,0:T(8,128)(2,1)S(1)}, u32[]{:S(2)}, u32[]{:S(2)}) collective-permute-start(bf16[32,1792]{1,0:T(8,128)(2,1)S(1)} %slice.647), channel_id=1, source_target_pairs={{0,4},{1,3},{2,6},{3,1},{4,0},{5,7},{6,2},{7,5},{8,12},{9,11},{10,... | collective-permute-start | bytes 344072 | tf_op jit(solution)/shard_map/ppermute | solution.py:168
  116.5 8.3 %collective-permute-start.29 = (bf16[32,1792]{1,0:T(8,128)(2,1)S(1)}, bf16[32,1792]{1,0:T(8,128)(2,1)S(1)}, u32[]{:S(2)}, u32[]{:S(2)}) collective-permute-start(bf16[32,1792]{1,0:T(8,128)(2,1)S(1)} %slice.646), channel_id=1, source_target_pairs={{0,4},{1,3},{2,6},{3,1},{4,0},{5,7},{6,2},{7,5},{8,12},{9,11},{10,... | collective-permute-start | bytes 344072 | tf_op jit(solution)/shard_map/ppermute | solution.py:168
  124.8 5.5 %collective-permute-start.30 = (bf16[16,1792]{1,0:T(8,128)(2,1)S(1)}, bf16[16,1792]{1,0:T(8,128)(2,1)S(1)}, u32[]{:S(2)}, u32[]{:S(2)}) collective-permute-start(bf16[16,1792]{1,0:T(8,128)(2,1)S(1)} %slice.650), channel_id=1, source_target_pairs={{0,2},{1,5},{2,0},{3,7},{4,6},{5,1},{6,4},{7,3},{8,10},{9,13},{10,... | collective-permute-start | bytes 172040 | tf_op jit(solution)/shard_map/ppermute | solution.py:168
  135.4 8.3 %collective-permute-start.22 = (bf16[32,1792]{1,0:T(8,128)(2,1)S(1)}, bf16[32,1792]{1,0:T(8,128)(2,1)S(1)}, u32[]{:S(2)}, u32[]{:S(2)}) collective-permute-start(bf16[32,1792]{1,0:T(8,128)(2,1)S(1)} %pad_maximum_fusion.12), channel_id=1, source_target_pairs={{0,4},{1,3},{2,6},{3,1},{4,0},{5,7},{6,2},{7,5},{8,12},{9,11},{10,... | collective-permute-start | bytes 344072 | tf_op jit(solution)/shard_map/ppermute | solution.py:168
  136.1 8.9 %collective-permute-start.32 = (bf16[32,1920]{1,0:T(8,128)(2,1)S(1)}, bf16[32,1920]{1,0:T(8,128)(2,1)S(1)}, u32[]{:S(2)}, u32[]{:S(2)}) collective-permute-start(bf16[32,1920]{1,0:T(8,128)(2,1)S(1)} %pad_maximum_fusion.9), channel_id=1, source_target_pairs={{0,4},{1,3},{2,6},{3,1},{4,0},{5,7},{6,2},{7,5},{8,12},{9,11},{10,... | collective-permute-start | bytes 368648 | tf_op jit(solution)/shard_map/ppermute | solution.py:168
  143.7 15.4 %collective-permute-start.23 = (bf16[64,1792]{1,0:T(8,128)(2,1)S(1)}, bf16[64,1792]{1,0:T(8,128)(2,1)S(1)}, u32[]{:S(2)}, u32[]{:S(2)}) collective-permute-start(bf16[64,1792]{1,0:T(8,128)(2,1)S(1)} %pad_maximum_fusion.8), channel_id=1, source_target_pairs={{0,8},{1,17},{2,10},{3,19},{4,12},{5,21},{6,14},{7,23},{8,0},{9,25... | collective-permute-start | bytes 688136 | tf_op jit(solution)/shard_map/ppermute | solution.py:168
  145.0 12.5 %collective-permute-start.33 = (bf16[64,1920]{1,0:T(8,128)(2,1)S(1)}, bf16[64,1920]{1,0:T(8,128)(2,1)S(1)}, u32[]{:S(2)}, u32[]{:S(2)}) collective-permute-start(bf16[64,1920]{1,0:T(8,128)(2,1)S(1)} %pad_maximum_fusion.4), channel_id=1, source_target_pairs={{0,8},{1,17},{2,10},{3,19},{4,12},{5,21},{6,14},{7,23},{8,0},{9,25... | collective-permute-start | bytes 737288 | tf_op jit(solution)/shard_map/ppermute | solution.py:168
  157.5 8.9 %collective-permute-start.34 = (bf16[128,1920]{1,0:T(8,128)(2,1)S(1)}, bf16[128,1920]{1,0:T(8,128)(2,1)S(1)}, u32[]{:S(2)}, u32[]{:S(2)}) collective-permute-start(bf16[128,1920]{1,0:T(8,128)(2,1)S(1)} %pad_maximum_fusion), channel_id=1, source_target_pairs={{0,16},{1,9},{2,18},{3,11},{4,20},{5,13},{6,22},{7,15},{8,24},{9,1... | collective-permute-start | bytes 1474568 | tf_op jit(solution)/shard_map/ppermute | solution.py:168
  159.2 12.2 %collective-permute-start.24 = (bf16[128,1792]{1,0:T(8,128)(2,1)S(1)}, bf16[128,1792]{1,0:T(8,128)(2,1)S(1)}, u32[]{:S(2)}, u32[]{:S(2)}) collective-permute-start(bf16[128,1792]{1,0:T(8,128)(2,1)S(1)} %pad_maximum_fusion.3), channel_id=1, source_target_pairs={{0,16},{1,9},{2,18},{3,11},{4,20},{5,13},{6,22},{7,15},{8,24},{9,1... | collective-permute-start | bytes 1376264 | tf_op jit(solution)/shard_map/ppermute | solution.py:168
  166.5 17.0 %collective-permute-start.35 = (bf16[256,1920]{1,0:T(8,128)(2,1)S(1)}, bf16[256,1920]{1,0:T(8,128)(2,1)}, u32[]{:S(2)}, u32[]{:S(2)}) collective-permute-start(bf16[256,1920]{1,0:T(8,128)(2,1)S(1)} %constant_dynamic-update-slice_fusion.15.rest_4_), channel_id=1, source_target_pairs={{0,1},{1,0},{2,3},{3,2},{4,5},{5,4},{6,7},{7,6},{8,9},{9,8},{10,11... | collective-permute-start | bytes 2949128 | tf_op jit(solution)/shard_map/ppermute | solution.py:159
  172.2 5.5 %collective-permute-start.25 = (bf16[256,1792]{1,0:T(8,128)(2,1)}, bf16[256,1792]{1,0:T(8,128)(2,1)}, u32[]{:S(2)}, u32[]{:S(2)}) collective-permute-start(bf16[256,1792]{1,0:T(8,128)(2,1)} %constant_dynamic-update-slice_fusion.10.near_ref), channel_id=1, source_target_pairs={{0,1},{1,0},{2,3},{3,2},{4,5},{5,4},{6,7},{7,6},{8,9},{9,8},{10,11... | collective-permute-start | bytes 2752520 | tf_op jit(solution)/shard_map/ppermute | solution.py:159
  (35 other events, 189.9 us)

commit v2 on v1

--- a/solution.py
+++ b/solution.py
@@ -82,13 +82,13 @@
 
 
 def grad_wdec(send, feat_ref, errs, wdec_ref, gbdec_ref, base, span, step):
-    near = errs[0].shape[0]
-    ones = jnp.ones((8, near), bf16)
+    tokens = errs[0].shape[0]
+    ones = jnp.ones((8, tokens), bf16)
     for low in range(0, span, step):
         cols = slice(low, min(low + step, span))
         value = sum(
-            dot(feat_ref[:, side * near : (side + 1) * near], err[:, cols], 1, 0)
-            for side, err in enumerate(errs)
+            dot(feat_ref[:, i * tokens : (i + 1) * tokens], err[:, cols], 1, 0)
+            for i, err in enumerate(errs)
         )
         send(value, wdec_ref.at[:, pl.ds(base + low, cols.stop - low)])
         gbdec_ref[:, cols] = sum(dot(ones, err[:, cols], 1, 0)[:1] for err in errs)
@@ -112,14 +112,19 @@
 def finish_body(
     step, entries, _, thr_ref, w_dec_ref, feat_ref, first_ref, second_ref, *rest
 ):
-    pre_refs, partial_refs, err_refs = rest[:2], rest[2:4], rest[4:6]
-    wenc_ref, wdec_ref, gthr_ref, gbenc_ref, gbdec_ref, loss_ref, buffer, sems = rest[6:]
+    pre_refs, partial_refs, err_refs = rest[:2], rest[2:4], rest[4:8]
+    wenc_ref, wdec_ref, gthr_ref, gbenc_ref, gbdec_ref, loss_ref = rest[8:14]
+    buffer, sems, whole_ref = rest[14:]
     span = first_ref.shape[0]
+    piece = err_refs[0].shape[0]
+    for i, err_ref in enumerate(err_refs):
+        whole_ref[i * piece : (i + 1) * piece, :] = err_ref[:, :span]
     send, drain = sender(buffer, sems)
     weight = w_dec_ref[:, span:]
     grads, sums_thr, sums_benc = [], 0.0, 0.0
-    for pre_ref, partial_ref, err_ref in zip(pre_refs, partial_refs, err_refs):
-        grad_feat = partial_ref[...] + dot(err_ref[:, :span], weight, 1, 1)
+    for side, (pre_ref, partial_ref) in enumerate(zip(pre_refs, partial_refs)):
+        rows = slice(2 * side * piece, 2 * (side + 1) * piece)
+        grad_feat = partial_ref[...] + dot(whole_ref[rows, :], weight, 1, 1)
         pre = pre_ref[...]
         soft = jax.nn.sigmoid((pre - thr_ref[...]) / gate_band)
         slope = soft * (1.0 - soft) / gate_band
@@ -141,7 +146,7 @@
             size = min(step, span - low)
             value = dot(layer_ref[low : low + size, :], grads, 1, 0)
             send(value, wenc_ref.at[pl.ds(i * span + low, size), :])
-    grad_wdec(send, feat_ref, err_refs, wdec_ref, gbdec_ref, span, span, step)
+    grad_wdec(send, feat_ref, (whole_ref,), wdec_ref, gbdec_ref, span, span, step)
     drain()
 
 
@@ -167,9 +172,11 @@
             pairs.append((d * n_mp + m, (d ^ dp_bits) * n_mp + (m ^ (2 * z_bits))))
         return lax.ppermute(value, both, pairs)
 
-    def gather(rows):
+    def gather(rows, apart=False):
         for step in range(steps):
             got = exchange(rows, step)
+            if apart and step == steps - 1:
+                return rows, got
             rows = jnp.concatenate([rows, got], axis=0)
         return rows
 
@@ -276,8 +283,12 @@
             rows = error.astype(bf16)
             if i == len(error_own) - 1:
                 rows = jnp.concatenate([rows, extra], axis=1)
-            near = gather(rows)
-            err_all.append((near, other_core(near)))
+            if i == len(error_own) - 1:
+                pieces = gather(rows, apart=True)
+                err_last = (*pieces, *(other_core(piece) for piece in pieces))
+            else:
+                near = gather(rows)
+                err_all.append((near, other_core(near)))
 
         vmem = pl.BlockSpec(memory_space=pltpu.VMEM)
         hbm = pl.BlockSpec(memory_space=pl.ANY)
@@ -317,10 +328,10 @@
                 jax.ShapeDtypeStruct((1, span), f32),
                 jax.ShapeDtypeStruct((1, 1), f32),
             ),
-            in_specs=[hbm] + [vmem] * 11,
+            in_specs=[hbm] + [vmem] * 13,
             out_specs=(hbm, hbm, vmem, vmem, vmem, pl.BlockSpec(memory_space=pltpu.SMEM)),
             input_output_aliases={0: 1},
-            scratch_shapes=scratch,
+            scratch_shapes=scratch + [pltpu.VMEM((2 * rows, span), bf16)],
             compiler_params=params,
             name="finish",
         )(
@@ -331,7 +342,7 @@
             *turned,
             *pre_act,
             *partial,
-            *err_all[1],
+            *err_last,
         )
         grad_bdec = jnp.concatenate([bdec_first, bdec_second], axis=1)[0]
         grad_thresh, grad_benc, loss_value = grad_thresh[0], grad_benc[0], loss[0, 0]

time: 193 us -> 187 us (0.969)
  waiting for transfers between devices: 89.1 us -> 81.1 us
  starting transfers between devices: 35.5 us -> 37.6 us
    ppermute x28, waiting for transfers between devices: 87.4 us -> 79.3 us  [exchange(): return lax.ppermute(value, both, pairs)]
    unnamed x58 -> x55, local copies, waits for them, and re-layouts: 11.9 us -> 11.8 us
  transfers between devices with their start and end apart: 36 -> 37, of which waited for: 24 -> 25; matrix products, arithmetic and copies ran while one was open for 5% -> 5% of each run, Pallas kernels for 4% -> 4%
where the time goes in v2:
time: 187 us
  waiting for transfers between devices  81.1 us (43%)
  starting transfers between devices  37.6 us (20%)
  blocking collectives  17.9 us (10%)
  matrix products  17 us (9%)
  Pallas kernels  15.2 us (8%)
  local copies, waits for them, and re-layouts  13.1 us (7%)
  other arithmetic  3.24 us (2%)
    ppermute x28, waiting for transfers between devices, exchange(): return lax.ppermute(value, both, pairs)  79.3 us
    ppermute x28, starting transfers between devices, exchange(): return lax.ppermute(value, both, pairs)  35.7 us
    all_gather x1, blocking collectives, whole_step(): full_rows = lax.all_gather(residual_in, 'mp', axis=1, tiled=True)  17.9 us
    dot_general x13, matrix products, dot(): lax.dot_general(left, right, (((left_dim,), (right_dim,)), ((), ())), pre...  17 us
    unnamed x55, local copies, waits for them, and re-layouts  11.8 us
    pallas_call x1, Pallas kernels, whole_step(): pl.pallas_call(functools.partial(finish_body, step, float(tokens * width)...  8.4 us
    pallas_call x1, Pallas kernels, whole_step(): pl.pallas_call(functools.partial(early_body, step), out_shape=(jax.ShapeD...  4.32 us
  transfers between devices with their start and end apart: 37, of which 25 were waited for; matrix products, arithmetic and copies ran while one was open for 5% of the time, Pallas kernels for 4%

profile of v2, /device:TPU:0, one launch (start us, length us, event | category | flops | bytes accessed | tf_op | source)
XLA Modules:
  0.0 186.5 jit_solution(17765498694364171793)
XLA Ops:
  0.9 17.9 %all_gather.3 = bf16[128,3584]{0,1:T(8,128)(2,1)S(1)} all-gather(bf16[128,448]{0,1:T(8,128)(2,1)} %param.11), channel_id=1, replica_groups=mesh['dp'=4,'mp'=8] {'mp'}, dimensions={1}, use_global_device_ids=true | all-gather | bytes 1032192 | tf_op jit(solution)/shard_map/all_gather | solution.py:203
  19.5 6.9 %fusion.61 = f32[128,1792]{1,0:T(8,128)S(1)} fusion(bf16[3584,1792]{1,0:T(8,128)(2,1)} %param.14, f32[128,3584]{1,0:T(8,128)S(1)} %get-tuple-element.48, f32[3584]{0:T(1024)S(1)} %copy-done.9, f32[128]{0:T(128)S(1)} %add_rsqrt_fusion.1), kind=kOutput, calls=%fused_computation.179 | convolution fusion | flops 1645543424 | bytes 15612416 | tf_op jit(solution)/shard_map/dot_general | solution.py:22
  27.3 2.2 %fusion.5 = bf16[128,1792]{1,0:T(8,128)(2,1)S(1)} fusion(bf16[3584,1792]{1,0:T(8,128)(2,1)S(1)} %bitcast.26, f32[128,1792]{1,0:T(8,128)S(1)} %fusion.61, f32[128,3584]{1,0:T(8,128)S(1)} %get-tuple-element.48, f32[3584]{0:T(1024)S(1)} %copy-done.9, f32[128]{0:T(128)S(1)} %add_rsqrt_fusion.1), kind=kOutput, calls=%fused_computation.9 | convolution fusion | flops 1647837184 | bytes 16071168 | tf_op jit(solution)/shard_map/dot_general | solution.py:22
  36.9 2.7 %collective-permute-done.4 = bf16[32,1792]{1,0:T(8,128)(2,1)S(1)} collective-permute-done((bf16[32,1792]{1,0:T(8,128)(2,1)S(1)}, bf16[32,1792]{1,0:T(8,128)(2,1)S(1)}, u32[]{:S(2)}, u32[]{:S(2)}) %collective-permute-start.4) | collective-permute-done | bytes 114720 | tf_op jit(solution)/shard_map/ppermute | solution.py:173
  39.7 3.0 %collective-permute-start.5 = (bf16[16,1792]{1,0:T(8,128)(2,1)S(1)}, bf16[16,1792]{1,0:T(8,128)(2,1)S(1)}, u32[]{:S(2)}, u32[]{:S(2)}) collective-permute-start(bf16[16,1792]{1,0:T(8,128)(2,1)S(1)} %slice.652), channel_id=1, source_target_pairs={{0,2},{1,5},{2,0},{3,7},{4,6},{5,1},{6,4},{7,3},{8,10},{9,13},{10,... | collective-permute-start | bytes 172040 | tf_op jit(solution)/shard_map/ppermute | solution.py:173
  51.5 2.9 %collective-permute-start.11 = (bf16[32,1792]{1,0:T(8,128)(2,1)S(1)}, bf16[32,1792]{1,0:T(8,128)(2,1)S(1)}, u32[]{:S(2)}, u32[]{:S(2)}) collective-permute-start(bf16[32,1792]{1,0:T(8,128)(2,1)S(1)} %pad_maximum_fusion.11), channel_id=1, source_target_pairs={{0,4},{1,3},{2,6},{3,1},{4,0},{5,7},{6,2},{7,5},{8,12},{9,11},{10,... | collective-permute-start | bytes 344072 | tf_op jit(solution)/shard_map/ppermute | solution.py:173
  54.4 2.4 %collective-permute-start.7 = (bf16[32,1792]{1,0:T(8,128)(2,1)S(1)}, bf16[32,1792]{1,0:T(8,128)(2,1)S(1)}, u32[]{:S(2)}, u32[]{:S(2)}) collective-permute-start(bf16[32,1792]{1,0:T(8,128)(2,1)S(1)} %pad_maximum_fusion.10), channel_id=1, source_target_pairs={{0,4},{1,3},{2,6},{3,1},{4,0},{5,7},{6,2},{7,5},{8,12},{9,11},{10,... | collective-permute-start | bytes 344072 | tf_op jit(solution)/shard_map/ppermute | solution.py:173
  58.9 3.0 %collective-permute-done.7 = bf16[32,1792]{1,0:T(8,128)(2,1)S(1)} collective-permute-done((bf16[32,1792]{1,0:T(8,128)(2,1)S(1)}, bf16[32,1792]{1,0:T(8,128)(2,1)S(1)}, u32[]{:S(2)}, u32[]{:S(2)}) %collective-permute-start.7) | collective-permute-done | bytes 114720 | tf_op jit(solution)/shard_map/ppermute | solution.py:173
  63.5 7.0 %collective-permute-done.8 = bf16[64,1792]{1,0:T(8,128)(2,1)S(1)} collective-permute-done((bf16[64,1792]{1,0:T(8,128)(2,1)S(1)}, bf16[64,1792]{1,0:T(8,128)(2,1)S(1)}, u32[]{:S(2)}, u32[]{:S(2)}) %collective-permute-start.8) | collective-permute-done | bytes 229408 | tf_op jit(solution)/shard_map/ppermute | solution.py:173
  72.7 6.3 %collective-permute-done.9 = bf16[128,1792]{1,0:T(8,128)(2,1)S(1)} collective-permute-done((bf16[128,1792]{1,0:T(8,128)(2,1)S(1)}, bf16[128,1792]{1,0:T(8,128)(2,1)S(1)}, u32[]{:S(2)}, u32[]{:S(2)}) %collective-permute-start.9) | collective-permute-done | bytes 458784 | tf_op jit(solution)/shard_map/ppermute | solution.py:173
  79.2 4.8 %collective-permute-done.13 = bf16[128,1792]{1,0:T(8,128)(2,1)S(1)} collective-permute-done((bf16[128,1792]{1,0:T(8,128)(2,1)S(1)}, bf16[128,1792]{1,0:T(8,128)(2,1)S(1)}, u32[]{:S(2)}, u32[]{:S(2)}) %collective-permute-start.13) | collective-permute-done | bytes 458784 | tf_op jit(solution)/shard_map/ppermute | solution.py:173
  97.2 5.7 %collective-permute-done.17 = bf16[128,1792]{1,0:T(8,128)(2,1)S(1)} collective-permute-done((bf16[128,1792]{1,0:T(8,128)(2,1)S(1)}, bf16[128,1792]{1,0:T(8,128)(2,1)S(1)}, u32[]{:S(2)}, u32[]{:S(2)}) %collective-permute-start.17) | collective-permute-done | bytes 458784 | tf_op jit(solution)/shard_map/ppermute | solution.py:173
  104.5 5.7 %collective-permute-done.27 = bf16[128,1792]{1,0:T(8,128)(2,1)S(1)} collective-permute-done((bf16[128,1792]{1,0:T(8,128)(2,1)S(1)}, bf16[128,1792]{1,0:T(8,128)(2,1)S(1)}, u32[]{:S(2)}, u32[]{:S(2)}) %collective-permute-start.27) | collective-permute-done | bytes 458784 | tf_op jit(solution)/shard_map/ppermute | solution.py:173
  112.0 4.4 %collective-permute-done.28 = bf16[64,1792]{1,0:T(8,128)(2,1)S(1)} collective-permute-done((bf16[64,1792]{1,0:T(8,128)(2,1)S(1)}, bf16[64,1792]{1,0:T(8,128)(2,1)S(1)}, u32[]{:S(2)}, u32[]{:S(2)}) %collective-permute-start.28) | collective-permute-done | bytes 229408 | tf_op jit(solution)/shard_map/ppermute | solution.py:173
  116.6 3.3 %collective-permute-done.19 = bf16[32,1792]{1,0:T(8,128)(2,1)S(1)} collective-permute-done((bf16[32,1792]{1,0:T(8,128)(2,1)S(1)}, bf16[32,1792]{1,0:T(8,128)(2,1)S(1)}, u32[]{:S(2)}, u32[]{:S(2)}) %collective-permute-start.19) | collective-permute-done | bytes 114720 | tf_op jit(solution)/shard_map/ppermute | solution.py:173
  120.3 4.5 %collective-permute-done.29 = bf16[32,1792]{1,0:T(8,128)(2,1)S(1)} collective-permute-done((bf16[32,1792]{1,0:T(8,128)(2,1)S(1)}, bf16[32,1792]{1,0:T(8,128)(2,1)S(1)}, u32[]{:S(2)}, u32[]{:S(2)}) %collective-permute-start.29) | collective-permute-done | bytes 114720 | tf_op jit(solution)/shard_map/ppermute | solution.py:173
  125.3 5.0 %collective-permute-done.30 = bf16[16,1792]{1,0:T(8,128)(2,1)S(1)} collective-permute-done((bf16[16,1792]{1,0:T(8,128)(2,1)S(1)}, bf16[16,1792]{1,0:T(8,128)(2,1)S(1)}, u32[]{:S(2)}, u32[]{:S(2)}) %collective-permute-start.30) | collective-permute-done | bytes 57376 | tf_op jit(solution)/shard_map/ppermute | solution.py:173
  136.1 3.0 %collective-permute-start.32 = (bf16[32,1920]{1,0:T(8,128)(2,1)S(1)}, bf16[32,1920]{1,0:T(8,128)(2,1)S(1)}, u32[]{:S(2)}, u32[]{:S(2)}) collective-permute-start(bf16[32,1920]{1,0:T(8,128)(2,1)S(1)} %pad_maximum_fusion.9), channel_id=1, source_target_pairs={{0,4},{1,3},{2,6},{3,1},{4,0},{5,7},{6,2},{7,5},{8,12},{9,11},{10,... | collective-permute-start | bytes 368648 | tf_op jit(solution)/shard_map/ppermute | solution.py:173
  139.1 4.6 %collective-permute-done.22 = bf16[32,1792]{1,0:T(8,128)(2,1)S(1)} collective-permute-done((bf16[32,1792]{1,0:T(8,128)(2,1)S(1)}, bf16[32,1792]{1,0:T(8,128)(2,1)S(1)}, u32[]{:S(2)}, u32[]{:S(2)}) %collective-permute-start.22) | collective-permute-done | bytes 114720 | tf_op jit(solution)/shard_map/ppermute | solution.py:173
  146.5 5.7 %collective-permute-done.23 = bf16[64,1792]{1,0:T(8,128)(2,1)S(1)} collective-permute-done((bf16[64,1792]{1,0:T(8,128)(2,1)S(1)}, bf16[64,1792]{1,0:T(8,128)(2,1)S(1)}, u32[]{:S(2)}, u32[]{:S(2)}) %collective-permute-start.23) | collective-permute-done | bytes 229408 | tf_op jit(solution)/shard_map/ppermute | solution.py:173
  157.9 2.9 %collective-permute-done.24 = bf16[128,1792]{1,0:T(8,128)(2,1)S(1)} collective-permute-done((bf16[128,1792]{1,0:T(8,128)(2,1)S(1)}, bf16[128,1792]{1,0:T(8,128)(2,1)S(1)}, u32[]{:S(2)}, u32[]{:S(2)}) %collective-permute-start.24) | collective-permute-done | bytes 458784 | tf_op jit(solution)/shard_map/ppermute | solution.py:173
  162.1 4.0 %collective-permute-done.34.rest_5_ = bf16[128,1920]{1,0:T(8,128)(2,1)S(1)} collective-permute-done((bf16[128,1920]{1,0:T(8,128)(2,1)S(1)}, bf16[128,1920]{1,0:T(8,128)(2,1)S(1)}, u32[]{:S(2)}, u32[]{:S(2)}) %collective-permute-start.34) | collective-permute-done | bytes 491552 | tf_op jit(solution)/shard_map/ppermute | solution.py:173
  173.1 4.3 %early.1 = (bf16[512,3584]{1,0:T(8,128)(2,1)}, f32[1,1792]{1,0:T(1,128)S(1)}, f32[256,512]{1,0:T(8,128)S(1)}, f32[256,512]{1,0:T(8,128)S(1)}) custom-call(bf16[512,512]{1,0:T(8,128)(2,1)S(1)} %turn.3.feat_ref, bf16[512,3584]{1,0:T(8,128)(2,1)S(1)} %copy-done.1, bf16[256,1792]{1,0:T(8,128)(2,1)} %constant_dynamic-update-slice_fusion.10.near_ref, ...), custom_call_target="tpu_custom_call" | custom-call | tf_op jit(solution)/shard_map/early/pallas_call | solution.py:307
  177.5 8.4 %finish.1 = (bf16[3584,512]{1,0:T(8,128)(2,1)}, bf16[512,3584]{1,0:T(8,128)(2,1)}, f32[1,512]{1,0:T(1,128)}, f32[1,512]{1,0:T(1,128)}, f32[1,1792]{1,0:T(1,128)S(1)}, /*index=5*/f32[1,1]{1,0:T(1,128)}) custom-call(bf16[512,3584]{1,0:T(8,128)(2,1)} %get-tuple-element.16._, f32[1,512]{1,0:T(1,128)S(1)} %copy-done.8, ...), custom_call_target="tpu_custom_call", output_to_operand_aliasing={{1}: (0, {})} | custom-call | tf_op jit(solution)/shard_map/finish/pallas_call | solution.py:321
  (191 shorter events, 64.7 us)
Async XLA Ops:
  33.8 5.9 %collective-permute-start.4 = (bf16[32,1792]{1,0:T(8,128)(2,1)S(1)}, bf16[32,1792]{1,0:T(8,128)(2,1)S(1)}, u32[]{:S(2)}, u32[]{:S(2)}) collective-permute-start(bf16[32,1792]{1,0:T(8,128)(2,1)S(1)} %slice.648), channel_id=1, source_target_pairs={{0,4},{1,3},{2,6},{3,1},{4,0},{5,7},{6,2},{7,5},{8,12},{9,11},{10,... | collective-permute-start | bytes 344072 | tf_op jit(solution)/shard_map/ppermute | solution.py:173
  35.1 7.6 %collective-permute-start.1 = (bf16[32,1792]{1,0:T(8,128)(2,1)S(1)}, bf16[32,1792]{1,0:T(8,128)(2,1)S(1)}, u32[]{:S(2)}, u32[]{:S(2)}) collective-permute-start(bf16[32,1792]{1,0:T(8,128)(2,1)S(1)} %slice.649), channel_id=1, source_target_pairs={{0,4},{1,3},{2,6},{3,1},{4,0},{5,7},{6,2},{7,5},{8,12},{9,11},{10,... | collective-permute-start | bytes 344072 | tf_op jit(solution)/shard_map/ppermute | solution.py:173
  51.5 5.8 %collective-permute-start.11 = (bf16[32,1792]{1,0:T(8,128)(2,1)S(1)}, bf16[32,1792]{1,0:T(8,128)(2,1)S(1)}, u32[]{:S(2)}, u32[]{:S(2)}) collective-permute-start(bf16[32,1792]{1,0:T(8,128)(2,1)S(1)} %pad_maximum_fusion.11), channel_id=1, source_target_pairs={{0,4},{1,3},{2,6},{3,1},{4,0},{5,7},{6,2},{7,5},{8,12},{9,11},{10,... | collective-permute-start | bytes 344072 | tf_op jit(solution)/shard_map/ppermute | solution.py:173
  54.4 7.5 %collective-permute-start.7 = (bf16[32,1792]{1,0:T(8,128)(2,1)S(1)}, bf16[32,1792]{1,0:T(8,128)(2,1)S(1)}, u32[]{:S(2)}, u32[]{:S(2)}) collective-permute-start(bf16[32,1792]{1,0:T(8,128)(2,1)S(1)} %pad_maximum_fusion.10), channel_id=1, source_target_pairs={{0,4},{1,3},{2,6},{3,1},{4,0},{5,7},{6,2},{7,5},{8,12},{9,11},{10,... | collective-permute-start | bytes 344072 | tf_op jit(solution)/shard_map/ppermute | solution.py:173
  57.3 14.8 %collective-permute-start.12 = (bf16[64,1792]{1,0:T(8,128)(2,1)S(1)}, bf16[64,1792]{1,0:T(8,128)(2,1)S(1)}, u32[]{:S(2)}, u32[]{:S(2)}) collective-permute-start(bf16[64,1792]{1,0:T(8,128)(2,1)S(1)} %pad_maximum_fusion.7), channel_id=1, source_target_pairs={{0,8},{1,17},{2,10},{3,19},{4,12},{5,21},{6,14},{7,23},{8,0},{9,25... | collective-permute-start | bytes 688136 | tf_op jit(solution)/shard_map/ppermute | solution.py:173
  61.9 8.5 %collective-permute-start.8 = (bf16[64,1792]{1,0:T(8,128)(2,1)S(1)}, bf16[64,1792]{1,0:T(8,128)(2,1)S(1)}, u32[]{:S(2)}, u32[]{:S(2)}) collective-permute-start(bf16[64,1792]{1,0:T(8,128)(2,1)S(1)} %pad_maximum_fusion.6), channel_id=1, source_target_pairs={{0,8},{1,17},{2,10},{3,19},{4,12},{5,21},{6,14},{7,23},{8,0},{9,25... | collective-permute-start | bytes 688136 | tf_op jit(solution)/shard_map/ppermute | solution.py:173
  70.5 8.5 %collective-permute-start.9 = (bf16[128,1792]{1,0:T(8,128)(2,1)S(1)}, bf16[128,1792]{1,0:T(8,128)(2,1)S(1)}, u32[]{:S(2)}, u32[]{:S(2)}) collective-permute-start(bf16[128,1792]{1,0:T(8,128)(2,1)S(1)} %pad_maximum_fusion.1), channel_id=1, source_target_pairs={{0,16},{1,9},{2,18},{3,11},{4,20},{5,13},{6,22},{7,15},{8,24},{9,1... | collective-permute-start | bytes 1376264 | tf_op jit(solution)/shard_map/ppermute | solution.py:173
  72.1 11.8 %collective-permute-start.13 = (bf16[128,1792]{1,0:T(8,128)(2,1)S(1)}, bf16[128,1792]{1,0:T(8,128)(2,1)S(1)}, u32[]{:S(2)}, u32[]{:S(2)}) collective-permute-start(bf16[128,1792]{1,0:T(8,128)(2,1)S(1)} %pad_maximum_fusion.2), channel_id=1, source_target_pairs={{0,16},{1,9},{2,18},{3,11},{4,20},{5,13},{6,22},{7,15},{8,24},{9,1... | collective-permute-start | bytes 1376264 | tf_op jit(solution)/shard_map/ppermute | solution.py:173
  79.1 6.5 %collective-permute-start.14 = (bf16[256,1792]{1,0:T(8,128)(2,1)S(1)}, bf16[256,1792]{1,0:T(8,128)(2,1)S(1)}, u32[]{:S(2)}, u32[]{:S(2)}) collective-permute-start(bf16[256,1792]{1,0:T(8,128)(2,1)S(1)} %constant_dynamic-update-slice_fusion.near_ref), channel_id=1, source_target_pairs={{0,1},{1,0},{2,3},{3,2},{4,5},{5,4},{6,7},{7,6},{8,9},{9,8},{10,11... | collective-permute-start | bytes 2752520 | tf_op jit(solution)/shard_map/ppermute | solution.py:164
  94.3 8.5 %collective-permute-start.17 = (bf16[128,1792]{1,0:T(8,128)(2,1)S(1)}, bf16[128,1792]{1,0:T(8,128)(2,1)S(1)}, u32[]{:S(2)}, u32[]{:S(2)}) collective-permute-start(bf16[128,1792]{1,0:T(8,128)(2,1)S(1)} %slice.641), channel_id=1, source_target_pairs={{0,16},{1,9},{2,18},{3,11},{4,20},{5,13},{6,22},{7,15},{8,24},{9,1... | collective-permute-start | bytes 1376264 | tf_op jit(solution)/shard_map/ppermute | solution.py:173
  96.6 13.6 %collective-permute-start.27 = (bf16[128,1792]{1,0:T(8,128)(2,1)S(1)}, bf16[128,1792]{1,0:T(8,128)(2,1)S(1)}, u32[]{:S(2)}, u32[]{:S(2)}) collective-permute-start(bf16[128,1792]{1,0:T(8,128)(2,1)S(1)} %slice.640), channel_id=1, source_target_pairs={{0,16},{1,9},{2,18},{3,11},{4,20},{5,13},{6,22},{7,15},{8,24},{9,1... | collective-permute-start | bytes 1376264 | tf_op jit(solution)/shard_map/ppermute | solution.py:173
  102.9 8.9 %collective-permute-start.18 = (bf16[64,1792]{1,0:T(8,128)(2,1)S(1)}, bf16[64,1792]{1,0:T(8,128)(2,1)S(1)}, u32[]{:S(2)}, u32[]{:S(2)}) collective-permute-start(bf16[64,1792]{1,0:T(8,128)(2,1)S(1)} %slice.643), channel_id=1, source_target_pairs={{0,8},{1,17},{2,10},{3,19},{4,12},{5,21},{6,14},{7,23},{8,0},{9,25... | collective-permute-start | bytes 688136 | tf_op jit(solution)/shard_map/ppermute | solution.py:173
  110.3 6.1 %collective-permute-start.28 = (bf16[64,1792]{1,0:T(8,128)(2,1)S(1)}, bf16[64,1792]{1,0:T(8,128)(2,1)S(1)}, u32[]{:S(2)}, u32[]{:S(2)}) collective-permute-start(bf16[64,1792]{1,0:T(8,128)(2,1)S(1)} %slice.642), channel_id=1, source_target_pairs={{0,8},{1,17},{2,10},{3,19},{4,12},{5,21},{6,14},{7,23},{8,0},{9,25... | collective-permute-start | bytes 688136 | tf_op jit(solution)/shard_map/ppermute | solution.py:173
  112.0 7.9 %collective-permute-start.19 = (bf16[32,1792]{1,0:T(8,128)(2,1)S(1)}, bf16[32,1792]{1,0:T(8,128)(2,1)S(1)}, u32[]{:S(2)}, u32[]{:S(2)}) collective-permute-start(bf16[32,1792]{1,0:T(8,128)(2,1)S(1)} %slice.647), channel_id=1, source_target_pairs={{0,4},{1,3},{2,6},{3,1},{4,0},{5,7},{6,2},{7,5},{8,12},{9,11},{10,... | collective-permute-start | bytes 344072 | tf_op jit(solution)/shard_map/ppermute | solution.py:173
  116.5 8.3 %collective-permute-start.29 = (bf16[32,1792]{1,0:T(8,128)(2,1)S(1)}, bf16[32,1792]{1,0:T(8,128)(2,1)S(1)}, u32[]{:S(2)}, u32[]{:S(2)}) collective-permute-start(bf16[32,1792]{1,0:T(8,128)(2,1)S(1)} %slice.646), channel_id=1, source_target_pairs={{0,4},{1,3},{2,6},{3,1},{4,0},{5,7},{6,2},{7,5},{8,12},{9,11},{10,... | collective-permute-start | bytes 344072 | tf_op jit(solution)/shard_map/ppermute | solution.py:173
  135.4 8.3 %collective-permute-start.22 = (bf16[32,1792]{1,0:T(8,128)(2,1)S(1)}, bf16[32,1792]{1,0:T(8,128)(2,1)S(1)}, u32[]{:S(2)}, u32[]{:S(2)}) collective-permute-start(bf16[32,1792]{1,0:T(8,128)(2,1)S(1)} %pad_maximum_fusion.12), channel_id=1, source_target_pairs={{0,4},{1,3},{2,6},{3,1},{4,0},{5,7},{6,2},{7,5},{8,12},{9,11},{10,... | collective-permute-start | bytes 344072 | tf_op jit(solution)/shard_map/ppermute | solution.py:173
  136.1 8.9 %collective-permute-start.32 = (bf16[32,1920]{1,0:T(8,128)(2,1)S(1)}, bf16[32,1920]{1,0:T(8,128)(2,1)S(1)}, u32[]{:S(2)}, u32[]{:S(2)}) collective-permute-start(bf16[32,1920]{1,0:T(8,128)(2,1)S(1)} %pad_maximum_fusion.9), channel_id=1, source_target_pairs={{0,4},{1,3},{2,6},{3,1},{4,0},{5,7},{6,2},{7,5},{8,12},{9,11},{10,... | collective-permute-start | bytes 368648 | tf_op jit(solution)/shard_map/ppermute | solution.py:173
  143.7 8.5 %collective-permute-start.23 = (bf16[64,1792]{1,0:T(8,128)(2,1)S(1)}, bf16[64,1792]{1,0:T(8,128)(2,1)S(1)}, u32[]{:S(2)}, u32[]{:S(2)}) collective-permute-start(bf16[64,1792]{1,0:T(8,128)(2,1)S(1)} %pad_maximum_fusion.8), channel_id=1, source_target_pairs={{0,8},{1,17},{2,10},{3,19},{4,12},{5,21},{6,14},{7,23},{8,0},{9,25... | collective-permute-start | bytes 688136 | tf_op jit(solution)/shard_map/ppermute | solution.py:173
  145.0 11.3 %collective-permute-start.33 = (bf16[64,1920]{1,0:T(8,128)(2,1)S(1)}, bf16[64,1920]{1,0:T(8,128)(2,1)S(1)}, u32[]{:S(2)}, u32[]{:S(2)}) collective-permute-start(bf16[64,1920]{1,0:T(8,128)(2,1)S(1)} %pad_maximum_fusion.4), channel_id=1, source_target_pairs={{0,8},{1,17},{2,10},{3,19},{4,12},{5,21},{6,14},{7,23},{8,0},{9,25... | collective-permute-start | bytes 737288 | tf_op jit(solution)/shard_map/ppermute | solution.py:173
  152.3 8.5 %collective-permute-start.24 = (bf16[128,1792]{1,0:T(8,128)(2,1)S(1)}, bf16[128,1792]{1,0:T(8,128)(2,1)S(1)}, u32[]{:S(2)}, u32[]{:S(2)}) collective-permute-start(bf16[128,1792]{1,0:T(8,128)(2,1)S(1)} %pad_maximum_fusion.3), channel_id=1, source_target_pairs={{0,16},{1,9},{2,18},{3,11},{4,20},{5,13},{6,22},{7,15},{8,24},{9,1... | collective-permute-start | bytes 1376264 | tf_op jit(solution)/shard_map/ppermute | solution.py:173
  156.3 9.7 %collective-permute-start.34 = (bf16[128,1920]{1,0:T(8,128)(2,1)S(1)}, bf16[128,1920]{1,0:T(8,128)(2,1)S(1)}, u32[]{:S(2)}, u32[]{:S(2)}) collective-permute-start(bf16[128,1920]{1,0:T(8,128)(2,1)S(1)} %pad_maximum_fusion.rest_4_), channel_id=1, source_target_pairs={{0,16},{1,9},{2,18},{3,11},{4,20},{5,13},{6,22},{7,15},{8,24},{9,1... | collective-permute-start | bytes 1474568 | tf_op jit(solution)/shard_map/ppermute | solution.py:173
  161.6 10.0 %collective-permute-start.25 = (bf16[256,1792]{1,0:T(8,128)(2,1)}, bf16[256,1792]{1,0:T(8,128)(2,1)}, u32[]{:S(2)}, u32[]{:S(2)}) collective-permute-start(bf16[256,1792]{1,0:T(8,128)(2,1)} %constant_dynamic-update-slice_fusion.10.near_ref), channel_id=1, source_target_pairs={{0,1},{1,0},{2,3},{3,2},{4,5},{5,4},{6,7},{7,6},{8,9},{9,8},{10,11... | collective-permute-start | bytes 2752520 | tf_op jit(solution)/shard_map/ppermute | solution.py:164
  161.6 15.8 %collective-permute-start.35 = (bf16[128,1920]{1,0:T(8,128)(2,1)S(1)}, bf16[128,1920]{1,0:T(8,128)(2,1)}, u32[]{:S(2)}, u32[]{:S(2)}) collective-permute-start(bf16[128,1920]{1,0:T(8,128)(2,1)S(1)} %pad_maximum_fusion.rest_4_), channel_id=1, source_target_pairs={{0,1},{1,0},{2,3},{3,2},{4,5},{5,4},{6,7},{7,6},{8,9},{9,8},{10,11... | collective-permute-start | bytes 1474568 | tf_op jit(solution)/shard_map/ppermute | solution.py:164
  166.1 11.4 %collective-permute-start.36 = (bf16[128,1920]{1,0:T(8,128)(2,1)S(1)}, bf16[128,1920]{1,0:T(8,128)(2,1)}, u32[]{:S(2)}, u32[]{:S(2)}) collective-permute-start(bf16[128,1920]{1,0:T(8,128)(2,1)S(1)} %collective-permute-done.34.rest_5_), channel_id=1, source_target_pairs={{0,1},{1,0},{2,3},{3,2},{4,5},{5,4},{6,7},{7,6},{8,9},{9,8},{10,11... | collective-permute-start | bytes 1474568 | tf_op jit(solution)/shard_map/ppermute | solution.py:164
  (36 other events, 195.4 us)

commit v3 on v2

--- a/solution.py
+++ b/solution.py
@@ -30,19 +30,19 @@
     turned_ref[:, count:] = far_ref[...].T
 
 
-def row_body(source_ref, row_ref):
+def row_body(source_ref, _, row_ref):
     row_ref[...] = source_ref[...]
 
 
-def row_of(values):
+def row_of(values, weight):
     vmem = pl.BlockSpec(memory_space=pltpu.VMEM)
     return pl.pallas_call(
         row_body,
         out_shape=jax.ShapeDtypeStruct((1, values.shape[0]), values.dtype),
-        in_specs=[vmem],
+        in_specs=[vmem, pl.BlockSpec(memory_space=pl.ANY)],
         out_specs=vmem,
         name="row",
-    )(values[None, :])
+    )(values[None, :], weight)
 
 
 def side_by_side(pair):
@@ -296,7 +296,7 @@
         turned = []
         for pair in layer_out:
             turned.append(side_by_side(pair))
-        threshold_row = row_of(threshold)
+        threshold_row = row_of(threshold, w_dec)
         feat_turned = side_by_side(feat)
         scratch = [
             pltpu.VMEM((4, max(step, features), max(step, features)), bf16),

time: 187 us -> 187 us (level)
  no operation moved by 1% of the time
where the time goes in v3:
time: 187 us
  waiting for transfers between devices  81.1 us (43%)
  starting transfers between devices  37.6 us (20%)
  blocking collectives  17.9 us (10%)
  matrix products  17 us (9%)
  Pallas kernels  15.2 us (8%)
  local copies, waits for them, and re-layouts  13.1 us (7%)
  other arithmetic  3.23 us (2%)
    ppermute x28, waiting for transfers between devices, exchange(): return lax.ppermute(value, both, pairs)  79.3 us
    ppermute x28, starting transfers between devices, exchange(): return lax.ppermute(value, both, pairs)  35.7 us
    all_gather x1, blocking collectives, whole_step(): full_rows = lax.all_gather(residual_in, 'mp', axis=1, tiled=True)  17.9 us
    dot_general x13, matrix products, dot(): lax.dot_general(left, right, (((left_dim,), (right_dim,)), ((), ())), pre...  17 us
    unnamed x55, local copies, waits for them, and re-layouts  11.8 us
    pallas_call x1, Pallas kernels, whole_step(): pl.pallas_call(functools.partial(finish_body, step, float(tokens * width)...  8.4 us
    pallas_call x1, Pallas kernels, whole_step(): pl.pallas_call(functools.partial(early_body, step), out_shape=(jax.ShapeD...  4.32 us
  transfers between devices with their start and end apart: 37, of which 25 were waited for; matrix products, arithmetic and copies ran while one was open for 5% of the time, Pallas kernels for 4%

profile of v3, /device:TPU:0, one launch (start us, length us, event | category | flops | bytes accessed | tf_op | source)
XLA Modules:
  0.0 186.5 jit_solution(11283777308336836906)
XLA Ops:
  0.9 17.9 %all_gather.3 = bf16[128,3584]{0,1:T(8,128)(2,1)S(1)} all-gather(bf16[128,448]{0,1:T(8,128)(2,1)} %param.11), channel_id=1, replica_groups=mesh['dp'=4,'mp'=8] {'mp'}, dimensions={1}, use_global_device_ids=true | all-gather | bytes 1032192 | tf_op jit(solution)/shard_map/all_gather | solution.py:203
  19.5 6.9 %fusion.61 = f32[128,1792]{1,0:T(8,128)S(1)} fusion(bf16[3584,1792]{1,0:T(8,128)(2,1)} %param.14, f32[128,3584]{1,0:T(8,128)S(1)} %get-tuple-element.48, f32[3584]{0:T(1024)S(1)} %copy-done.9, f32[128]{0:T(128)S(1)} %add_rsqrt_fusion.1), kind=kOutput, calls=%fused_computation.179 | convolution fusion | flops 1645543424 | bytes 15612416 | tf_op jit(solution)/shard_map/dot_general | solution.py:22
  27.3 2.2 %fusion.5 = bf16[128,1792]{1,0:T(8,128)(2,1)S(1)} fusion(bf16[3584,1792]{1,0:T(8,128)(2,1)S(1)} %bitcast.26, f32[128,1792]{1,0:T(8,128)S(1)} %fusion.61, f32[128,3584]{1,0:T(8,128)S(1)} %get-tuple-element.48, f32[3584]{0:T(1024)S(1)} %copy-done.9, f32[128]{0:T(128)S(1)} %add_rsqrt_fusion.1), kind=kOutput, calls=%fused_computation.9 | convolution fusion | flops 1647837184 | bytes 16071168 | tf_op jit(solution)/shard_map/dot_general | solution.py:22
  36.9 2.7 %collective-permute-done.4 = bf16[32,1792]{1,0:T(8,128)(2,1)S(1)} collective-permute-done((bf16[32,1792]{1,0:T(8,128)(2,1)S(1)}, bf16[32,1792]{1,0:T(8,128)(2,1)S(1)}, u32[]{:S(2)}, u32[]{:S(2)}) %collective-permute-start.4) | collective-permute-done | bytes 114720 | tf_op jit(solution)/shard_map/ppermute | solution.py:173
  39.7 3.0 %collective-permute-start.5 = (bf16[16,1792]{1,0:T(8,128)(2,1)S(1)}, bf16[16,1792]{1,0:T(8,128)(2,1)S(1)}, u32[]{:S(2)}, u32[]{:S(2)}) collective-permute-start(bf16[16,1792]{1,0:T(8,128)(2,1)S(1)} %slice.652), channel_id=1, source_target_pairs={{0,2},{1,5},{2,0},{3,7},{4,6},{5,1},{6,4},{7,3},{8,10},{9,13},{10,... | collective-permute-start | bytes 172040 | tf_op jit(solution)/shard_map/ppermute | solution.py:173
  51.5 2.9 %collective-permute-start.11 = (bf16[32,1792]{1,0:T(8,128)(2,1)S(1)}, bf16[32,1792]{1,0:T(8,128)(2,1)S(1)}, u32[]{:S(2)}, u32[]{:S(2)}) collective-permute-start(bf16[32,1792]{1,0:T(8,128)(2,1)S(1)} %pad_maximum_fusion.11), channel_id=1, source_target_pairs={{0,4},{1,3},{2,6},{3,1},{4,0},{5,7},{6,2},{7,5},{8,12},{9,11},{10,... | collective-permute-start | bytes 344072 | tf_op jit(solution)/shard_map/ppermute | solution.py:173
  54.4 2.4 %collective-permute-start.7 = (bf16[32,1792]{1,0:T(8,128)(2,1)S(1)}, bf16[32,1792]{1,0:T(8,128)(2,1)S(1)}, u32[]{:S(2)}, u32[]{:S(2)}) collective-permute-start(bf16[32,1792]{1,0:T(8,128)(2,1)S(1)} %pad_maximum_fusion.10), channel_id=1, source_target_pairs={{0,4},{1,3},{2,6},{3,1},{4,0},{5,7},{6,2},{7,5},{8,12},{9,11},{10,... | collective-permute-start | bytes 344072 | tf_op jit(solution)/shard_map/ppermute | solution.py:173
  58.9 3.0 %collective-permute-done.7 = bf16[32,1792]{1,0:T(8,128)(2,1)S(1)} collective-permute-done((bf16[32,1792]{1,0:T(8,128)(2,1)S(1)}, bf16[32,1792]{1,0:T(8,128)(2,1)S(1)}, u32[]{:S(2)}, u32[]{:S(2)}) %collective-permute-start.7) | collective-permute-done | bytes 114720 | tf_op jit(solution)/shard_map/ppermute | solution.py:173
  63.5 7.0 %collective-permute-done.8 = bf16[64,1792]{1,0:T(8,128)(2,1)S(1)} collective-permute-done((bf16[64,1792]{1,0:T(8,128)(2,1)S(1)}, bf16[64,1792]{1,0:T(8,128)(2,1)S(1)}, u32[]{:S(2)}, u32[]{:S(2)}) %collective-permute-start.8) | collective-permute-done | bytes 229408 | tf_op jit(solution)/shard_map/ppermute | solution.py:173
  72.7 6.3 %collective-permute-done.9 = bf16[128,1792]{1,0:T(8,128)(2,1)S(1)} collective-permute-done((bf16[128,1792]{1,0:T(8,128)(2,1)S(1)}, bf16[128,1792]{1,0:T(8,128)(2,1)S(1)}, u32[]{:S(2)}, u32[]{:S(2)}) %collective-permute-start.9) | collective-permute-done | bytes 458784 | tf_op jit(solution)/shard_map/ppermute | solution.py:173
  79.2 4.8 %collective-permute-done.13 = bf16[128,1792]{1,0:T(8,128)(2,1)S(1)} collective-permute-done((bf16[128,1792]{1,0:T(8,128)(2,1)S(1)}, bf16[128,1792]{1,0:T(8,128)(2,1)S(1)}, u32[]{:S(2)}, u32[]{:S(2)}) %collective-permute-start.13) | collective-permute-done | bytes 458784 | tf_op jit(solution)/shard_map/ppermute | solution.py:173
  97.2 5.7 %collective-permute-done.17 = bf16[128,1792]{1,0:T(8,128)(2,1)S(1)} collective-permute-done((bf16[128,1792]{1,0:T(8,128)(2,1)S(1)}, bf16[128,1792]{1,0:T(8,128)(2,1)S(1)}, u32[]{:S(2)}, u32[]{:S(2)}) %collective-permute-start.17) | collective-permute-done | bytes 458784 | tf_op jit(solution)/shard_map/ppermute | solution.py:173
  104.5 5.7 %collective-permute-done.27 = bf16[128,1792]{1,0:T(8,128)(2,1)S(1)} collective-permute-done((bf16[128,1792]{1,0:T(8,128)(2,1)S(1)}, bf16[128,1792]{1,0:T(8,128)(2,1)S(1)}, u32[]{:S(2)}, u32[]{:S(2)}) %collective-permute-start.27) | collective-permute-done | bytes 458784 | tf_op jit(solution)/shard_map/ppermute | solution.py:173
  112.0 4.4 %collective-permute-done.28 = bf16[64,1792]{1,0:T(8,128)(2,1)S(1)} collective-permute-done((bf16[64,1792]{1,0:T(8,128)(2,1)S(1)}, bf16[64,1792]{1,0:T(8,128)(2,1)S(1)}, u32[]{:S(2)}, u32[]{:S(2)}) %collective-permute-start.28) | collective-permute-done | bytes 229408 | tf_op jit(solution)/shard_map/ppermute | solution.py:173
  116.6 3.3 %collective-permute-done.19 = bf16[32,1792]{1,0:T(8,128)(2,1)S(1)} collective-permute-done((bf16[32,1792]{1,0:T(8,128)(2,1)S(1)}, bf16[32,1792]{1,0:T(8,128)(2,1)S(1)}, u32[]{:S(2)}, u32[]{:S(2)}) %collective-permute-start.19) | collective-permute-done | bytes 114720 | tf_op jit(solution)/shard_map/ppermute | solution.py:173
  120.3 4.5 %collective-permute-done.29 = bf16[32,1792]{1,0:T(8,128)(2,1)S(1)} collective-permute-done((bf16[32,1792]{1,0:T(8,128)(2,1)S(1)}, bf16[32,1792]{1,0:T(8,128)(2,1)S(1)}, u32[]{:S(2)}, u32[]{:S(2)}) %collective-permute-start.29) | collective-permute-done | bytes 114720 | tf_op jit(solution)/shard_map/ppermute | solution.py:173
  125.3 5.0 %collective-permute-done.30 = bf16[16,1792]{1,0:T(8,128)(2,1)S(1)} collective-permute-done((bf16[16,1792]{1,0:T(8,128)(2,1)S(1)}, bf16[16,1792]{1,0:T(8,128)(2,1)S(1)}, u32[]{:S(2)}, u32[]{:S(2)}) %collective-permute-start.30) | collective-permute-done | bytes 57376 | tf_op jit(solution)/shard_map/ppermute | solution.py:173
  136.1 3.0 %collective-permute-start.32 = (bf16[32,1920]{1,0:T(8,128)(2,1)S(1)}, bf16[32,1920]{1,0:T(8,128)(2,1)S(1)}, u32[]{:S(2)}, u32[]{:S(2)}) collective-permute-start(bf16[32,1920]{1,0:T(8,128)(2,1)S(1)} %pad_maximum_fusion.9), channel_id=1, source_target_pairs={{0,4},{1,3},{2,6},{3,1},{4,0},{5,7},{6,2},{7,5},{8,12},{9,11},{10,... | collective-permute-start | bytes 368648 | tf_op jit(solution)/shard_map/ppermute | solution.py:173
  139.1 4.6 %collective-permute-done.22 = bf16[32,1792]{1,0:T(8,128)(2,1)S(1)} collective-permute-done((bf16[32,1792]{1,0:T(8,128)(2,1)S(1)}, bf16[32,1792]{1,0:T(8,128)(2,1)S(1)}, u32[]{:S(2)}, u32[]{:S(2)}) %collective-permute-start.22) | collective-permute-done | bytes 114720 | tf_op jit(solution)/shard_map/ppermute | solution.py:173
  146.5 5.7 %collective-permute-done.23 = bf16[64,1792]{1,0:T(8,128)(2,1)S(1)} collective-permute-done((bf16[64,1792]{1,0:T(8,128)(2,1)S(1)}, bf16[64,1792]{1,0:T(8,128)(2,1)S(1)}, u32[]{:S(2)}, u32[]{:S(2)}) %collective-permute-start.23) | collective-permute-done | bytes 229408 | tf_op jit(solution)/shard_map/ppermute | solution.py:173
  157.9 2.9 %collective-permute-done.24 = bf16[128,1792]{1,0:T(8,128)(2,1)S(1)} collective-permute-done((bf16[128,1792]{1,0:T(8,128)(2,1)S(1)}, bf16[128,1792]{1,0:T(8,128)(2,1)S(1)}, u32[]{:S(2)}, u32[]{:S(2)}) %collective-permute-start.24) | collective-permute-done | bytes 458784 | tf_op jit(solution)/shard_map/ppermute | solution.py:173
  162.1 4.0 %collective-permute-done.34.rest_5_ = bf16[128,1920]{1,0:T(8,128)(2,1)S(1)} collective-permute-done((bf16[128,1920]{1,0:T(8,128)(2,1)S(1)}, bf16[128,1920]{1,0:T(8,128)(2,1)S(1)}, u32[]{:S(2)}, u32[]{:S(2)}) %collective-permute-start.34) | collective-permute-done | bytes 491552 | tf_op jit(solution)/shard_map/ppermute | solution.py:173
  173.1 4.3 %early.1 = (bf16[512,3584]{1,0:T(8,128)(2,1)}, f32[1,1792]{1,0:T(1,128)S(1)}, f32[256,512]{1,0:T(8,128)S(1)}, f32[256,512]{1,0:T(8,128)S(1)}) custom-call(bf16[512,512]{1,0:T(8,128)(2,1)S(1)} %turn.3.feat_ref, bf16[512,3584]{1,0:T(8,128)(2,1)S(1)} %copy-done.1, bf16[256,1792]{1,0:T(8,128)(2,1)} %constant_dynamic-update-slice_fusion.10.near_ref, ...), custom_call_target="tpu_custom_call" | custom-call | tf_op jit(solution)/shard_map/early/pallas_call | solution.py:307
  177.5 8.4 %finish.1 = (bf16[3584,512]{1,0:T(8,128)(2,1)}, bf16[512,3584]{1,0:T(8,128)(2,1)}, f32[1,512]{1,0:T(1,128)}, f32[1,512]{1,0:T(1,128)}, f32[1,1792]{1,0:T(1,128)S(1)}, /*index=5*/f32[1,1]{1,0:T(1,128)}) custom-call(bf16[512,3584]{1,0:T(8,128)(2,1)} %get-tuple-element.16._, f32[1,512]{1,0:T(1,128)S(1)} %copy-done.8, ...), custom_call_target="tpu_custom_call", output_to_operand_aliasing={{1}: (0, {})} | custom-call | tf_op jit(solution)/shard_map/finish/pallas_call | solution.py:321
  (191 shorter events, 64.7 us)
Async XLA Ops:
  33.8 5.9 %collective-permute-start.4 = (bf16[32,1792]{1,0:T(8,128)(2,1)S(1)}, bf16[32,1792]{1,0:T(8,128)(2,1)S(1)}, u32[]{:S(2)}, u32[]{:S(2)}) collective-permute-start(bf16[32,1792]{1,0:T(8,128)(2,1)S(1)} %slice.648), channel_id=1, source_target_pairs={{0,4},{1,3},{2,6},{3,1},{4,0},{5,7},{6,2},{7,5},{8,12},{9,11},{10,... | collective-permute-start | bytes 344072 | tf_op jit(solution)/shard_map/ppermute | solution.py:173
  35.1 7.6 %collective-permute-start.1 = (bf16[32,1792]{1,0:T(8,128)(2,1)S(1)}, bf16[32,1792]{1,0:T(8,128)(2,1)S(1)}, u32[]{:S(2)}, u32[]{:S(2)}) collective-permute-start(bf16[32,1792]{1,0:T(8,128)(2,1)S(1)} %slice.649), channel_id=1, source_target_pairs={{0,4},{1,3},{2,6},{3,1},{4,0},{5,7},{6,2},{7,5},{8,12},{9,11},{10,... | collective-permute-start | bytes 344072 | tf_op jit(solution)/shard_map/ppermute | solution.py:173
  51.5 5.8 %collective-permute-start.11 = (bf16[32,1792]{1,0:T(8,128)(2,1)S(1)}, bf16[32,1792]{1,0:T(8,128)(2,1)S(1)}, u32[]{:S(2)}, u32[]{:S(2)}) collective-permute-start(bf16[32,1792]{1,0:T(8,128)(2,1)S(1)} %pad_maximum_fusion.11), channel_id=1, source_target_pairs={{0,4},{1,3},{2,6},{3,1},{4,0},{5,7},{6,2},{7,5},{8,12},{9,11},{10,... | collective-permute-start | bytes 344072 | tf_op jit(solution)/shard_map/ppermute | solution.py:173
  54.4 7.5 %collective-permute-start.7 = (bf16[32,1792]{1,0:T(8,128)(2,1)S(1)}, bf16[32,1792]{1,0:T(8,128)(2,1)S(1)}, u32[]{:S(2)}, u32[]{:S(2)}) collective-permute-start(bf16[32,1792]{1,0:T(8,128)(2,1)S(1)} %pad_maximum_fusion.10), channel_id=1, source_target_pairs={{0,4},{1,3},{2,6},{3,1},{4,0},{5,7},{6,2},{7,5},{8,12},{9,11},{10,... | collective-permute-start | bytes 344072 | tf_op jit(solution)/shard_map/ppermute | solution.py:173
  57.3 14.8 %collective-permute-start.12 = (bf16[64,1792]{1,0:T(8,128)(2,1)S(1)}, bf16[64,1792]{1,0:T(8,128)(2,1)S(1)}, u32[]{:S(2)}, u32[]{:S(2)}) collective-permute-start(bf16[64,1792]{1,0:T(8,128)(2,1)S(1)} %pad_maximum_fusion.7), channel_id=1, source_target_pairs={{0,8},{1,17},{2,10},{3,19},{4,12},{5,21},{6,14},{7,23},{8,0},{9,25... | collective-permute-start | bytes 688136 | tf_op jit(solution)/shard_map/ppermute | solution.py:173
  61.9 8.5 %collective-permute-start.8 = (bf16[64,1792]{1,0:T(8,128)(2,1)S(1)}, bf16[64,1792]{1,0:T(8,128)(2,1)S(1)}, u32[]{:S(2)}, u32[]{:S(2)}) collective-permute-start(bf16[64,1792]{1,0:T(8,128)(2,1)S(1)} %pad_maximum_fusion.6), channel_id=1, source_target_pairs={{0,8},{1,17},{2,10},{3,19},{4,12},{5,21},{6,14},{7,23},{8,0},{9,25... | collective-permute-start | bytes 688136 | tf_op jit(solution)/shard_map/ppermute | solution.py:173
  70.5 8.5 %collective-permute-start.9 = (bf16[128,1792]{1,0:T(8,128)(2,1)S(1)}, bf16[128,1792]{1,0:T(8,128)(2,1)S(1)}, u32[]{:S(2)}, u32[]{:S(2)}) collective-permute-start(bf16[128,1792]{1,0:T(8,128)(2,1)S(1)} %pad_maximum_fusion.1), channel_id=1, source_target_pairs={{0,16},{1,9},{2,18},{3,11},{4,20},{5,13},{6,22},{7,15},{8,24},{9,1... | collective-permute-start | bytes 1376264 | tf_op jit(solution)/shard_map/ppermute | solution.py:173
  72.1 11.8 %collective-permute-start.13 = (bf16[128,1792]{1,0:T(8,128)(2,1)S(1)}, bf16[128,1792]{1,0:T(8,128)(2,1)S(1)}, u32[]{:S(2)}, u32[]{:S(2)}) collective-permute-start(bf16[128,1792]{1,0:T(8,128)(2,1)S(1)} %pad_maximum_fusion.2), channel_id=1, source_target_pairs={{0,16},{1,9},{2,18},{3,11},{4,20},{5,13},{6,22},{7,15},{8,24},{9,1... | collective-permute-start | bytes 1376264 | tf_op jit(solution)/shard_map/ppermute | solution.py:173
  79.1 6.5 %collective-permute-start.14 = (bf16[256,1792]{1,0:T(8,128)(2,1)S(1)}, bf16[256,1792]{1,0:T(8,128)(2,1)S(1)}, u32[]{:S(2)}, u32[]{:S(2)}) collective-permute-start(bf16[256,1792]{1,0:T(8,128)(2,1)S(1)} %constant_dynamic-update-slice_fusion.near_ref), channel_id=1, source_target_pairs={{0,1},{1,0},{2,3},{3,2},{4,5},{5,4},{6,7},{7,6},{8,9},{9,8},{10,11... | collective-permute-start | bytes 2752520 | tf_op jit(solution)/shard_map/ppermute | solution.py:164
  94.3 8.5 %collective-permute-start.17 = (bf16[128,1792]{1,0:T(8,128)(2,1)S(1)}, bf16[128,1792]{1,0:T(8,128)(2,1)S(1)}, u32[]{:S(2)}, u32[]{:S(2)}) collective-permute-start(bf16[128,1792]{1,0:T(8,128)(2,1)S(1)} %slice.641), channel_id=1, source_target_pairs={{0,16},{1,9},{2,18},{3,11},{4,20},{5,13},{6,22},{7,15},{8,24},{9,1... | collective-permute-start | bytes 1376264 | tf_op jit(solution)/shard_map/ppermute | solution.py:173
  96.6 13.6 %collective-permute-start.27 = (bf16[128,1792]{1,0:T(8,128)(2,1)S(1)}, bf16[128,1792]{1,0:T(8,128)(2,1)S(1)}, u32[]{:S(2)}, u32[]{:S(2)}) collective-permute-start(bf16[128,1792]{1,0:T(8,128)(2,1)S(1)} %slice.640), channel_id=1, source_target_pairs={{0,16},{1,9},{2,18},{3,11},{4,20},{5,13},{6,22},{7,15},{8,24},{9,1... | collective-permute-start | bytes 1376264 | tf_op jit(solution)/shard_map/ppermute | solution.py:173
  102.9 8.9 %collective-permute-start.18 = (bf16[64,1792]{1,0:T(8,128)(2,1)S(1)}, bf16[64,1792]{1,0:T(8,128)(2,1)S(1)}, u32[]{:S(2)}, u32[]{:S(2)}) collective-permute-start(bf16[64,1792]{1,0:T(8,128)(2,1)S(1)} %slice.643), channel_id=1, source_target_pairs={{0,8},{1,17},{2,10},{3,19},{4,12},{5,21},{6,14},{7,23},{8,0},{9,25... | collective-permute-start | bytes 688136 | tf_op jit(solution)/shard_map/ppermute | solution.py:173
  110.3 6.1 %collective-permute-start.28 = (bf16[64,1792]{1,0:T(8,128)(2,1)S(1)}, bf16[64,1792]{1,0:T(8,128)(2,1)S(1)}, u32[]{:S(2)}, u32[]{:S(2)}) collective-permute-start(bf16[64,1792]{1,0:T(8,128)(2,1)S(1)} %slice.642), channel_id=1, source_target_pairs={{0,8},{1,17},{2,10},{3,19},{4,12},{5,21},{6,14},{7,23},{8,0},{9,25... | collective-permute-start | bytes 688136 | tf_op jit(solution)/shard_map/ppermute | solution.py:173
  112.0 7.9 %collective-permute-start.19 = (bf16[32,1792]{1,0:T(8,128)(2,1)S(1)}, bf16[32,1792]{1,0:T(8,128)(2,1)S(1)}, u32[]{:S(2)}, u32[]{:S(2)}) collective-permute-start(bf16[32,1792]{1,0:T(8,128)(2,1)S(1)} %slice.647), channel_id=1, source_target_pairs={{0,4},{1,3},{2,6},{3,1},{4,0},{5,7},{6,2},{7,5},{8,12},{9,11},{10,... | collective-permute-start | bytes 344072 | tf_op jit(solution)/shard_map/ppermute | solution.py:173
  116.5 8.3 %collective-permute-start.29 = (bf16[32,1792]{1,0:T(8,128)(2,1)S(1)}, bf16[32,1792]{1,0:T(8,128)(2,1)S(1)}, u32[]{:S(2)}, u32[]{:S(2)}) collective-permute-start(bf16[32,1792]{1,0:T(8,128)(2,1)S(1)} %slice.646), channel_id=1, source_target_pairs={{0,4},{1,3},{2,6},{3,1},{4,0},{5,7},{6,2},{7,5},{8,12},{9,11},{10,... | collective-permute-start | bytes 344072 | tf_op jit(solution)/shard_map/ppermute | solution.py:173
  135.4 8.3 %collective-permute-start.22 = (bf16[32,1792]{1,0:T(8,128)(2,1)S(1)}, bf16[32,1792]{1,0:T(8,128)(2,1)S(1)}, u32[]{:S(2)}, u32[]{:S(2)}) collective-permute-start(bf16[32,1792]{1,0:T(8,128)(2,1)S(1)} %pad_maximum_fusion.12), channel_id=1, source_target_pairs={{0,4},{1,3},{2,6},{3,1},{4,0},{5,7},{6,2},{7,5},{8,12},{9,11},{10,... | collective-permute-start | bytes 344072 | tf_op jit(solution)/shard_map/ppermute | solution.py:173
  136.1 8.9 %collective-permute-start.32 = (bf16[32,1920]{1,0:T(8,128)(2,1)S(1)}, bf16[32,1920]{1,0:T(8,128)(2,1)S(1)}, u32[]{:S(2)}, u32[]{:S(2)}) collective-permute-start(bf16[32,1920]{1,0:T(8,128)(2,1)S(1)} %pad_maximum_fusion.9), channel_id=1, source_target_pairs={{0,4},{1,3},{2,6},{3,1},{4,0},{5,7},{6,2},{7,5},{8,12},{9,11},{10,... | collective-permute-start | bytes 368648 | tf_op jit(solution)/shard_map/ppermute | solution.py:173
  143.7 8.5 %collective-permute-start.23 = (bf16[64,1792]{1,0:T(8,128)(2,1)S(1)}, bf16[64,1792]{1,0:T(8,128)(2,1)S(1)}, u32[]{:S(2)}, u32[]{:S(2)}) collective-permute-start(bf16[64,1792]{1,0:T(8,128)(2,1)S(1)} %pad_maximum_fusion.8), channel_id=1, source_target_pairs={{0,8},{1,17},{2,10},{3,19},{4,12},{5,21},{6,14},{7,23},{8,0},{9,25... | collective-permute-start | bytes 688136 | tf_op jit(solution)/shard_map/ppermute | solution.py:173
  145.0 11.3 %collective-permute-start.33 = (bf16[64,1920]{1,0:T(8,128)(2,1)S(1)}, bf16[64,1920]{1,0:T(8,128)(2,1)S(1)}, u32[]{:S(2)}, u32[]{:S(2)}) collective-permute-start(bf16[64,1920]{1,0:T(8,128)(2,1)S(1)} %pad_maximum_fusion.4), channel_id=1, source_target_pairs={{0,8},{1,17},{2,10},{3,19},{4,12},{5,21},{6,14},{7,23},{8,0},{9,25... | collective-permute-start | bytes 737288 | tf_op jit(solution)/shard_map/ppermute | solution.py:173
  152.3 8.5 %collective-permute-start.24 = (bf16[128,1792]{1,0:T(8,128)(2,1)S(1)}, bf16[128,1792]{1,0:T(8,128)(2,1)S(1)}, u32[]{:S(2)}, u32[]{:S(2)}) collective-permute-start(bf16[128,1792]{1,0:T(8,128)(2,1)S(1)} %pad_maximum_fusion.3), channel_id=1, source_target_pairs={{0,16},{1,9},{2,18},{3,11},{4,20},{5,13},{6,22},{7,15},{8,24},{9,1... | collective-permute-start | bytes 1376264 | tf_op jit(solution)/shard_map/ppermute | solution.py:173
  156.3 9.7 %collective-permute-start.34 = (bf16[128,1920]{1,0:T(8,128)(2,1)S(1)}, bf16[128,1920]{1,0:T(8,128)(2,1)S(1)}, u32[]{:S(2)}, u32[]{:S(2)}) collective-permute-start(bf16[128,1920]{1,0:T(8,128)(2,1)S(1)} %pad_maximum_fusion.rest_4_), channel_id=1, source_target_pairs={{0,16},{1,9},{2,18},{3,11},{4,20},{5,13},{6,22},{7,15},{8,24},{9,1... | collective-permute-start | bytes 1474568 | tf_op jit(solution)/shard_map/ppermute | solution.py:173
  161.6 10.0 %collective-permute-start.25 = (bf16[256,1792]{1,0:T(8,128)(2,1)}, bf16[256,1792]{1,0:T(8,128)(2,1)}, u32[]{:S(2)}, u32[]{:S(2)}) collective-permute-start(bf16[256,1792]{1,0:T(8,128)(2,1)} %constant_dynamic-update-slice_fusion.10.near_ref), channel_id=1, source_target_pairs={{0,1},{1,0},{2,3},{3,2},{4,5},{5,4},{6,7},{7,6},{8,9},{9,8},{10,11... | collective-permute-start | bytes 2752520 | tf_op jit(solution)/shard_map/ppermute | solution.py:164
  161.6 15.8 %collective-permute-start.35 = (bf16[128,1920]{1,0:T(8,128)(2,1)S(1)}, bf16[128,1920]{1,0:T(8,128)(2,1)}, u32[]{:S(2)}, u32[]{:S(2)}) collective-permute-start(bf16[128,1920]{1,0:T(8,128)(2,1)S(1)} %pad_maximum_fusion.rest_4_), channel_id=1, source_target_pairs={{0,1},{1,0},{2,3},{3,2},{4,5},{5,4},{6,7},{7,6},{8,9},{9,8},{10,11... | collective-permute-start | bytes 1474568 | tf_op jit(solution)/shard_map/ppermute | solution.py:164
  166.1 11.4 %collective-permute-start.36 = (bf16[128,1920]{1,0:T(8,128)(2,1)S(1)}, bf16[128,1920]{1,0:T(8,128)(2,1)}, u32[]{:S(2)}, u32[]{:S(2)}) collective-permute-start(bf16[128,1920]{1,0:T(8,128)(2,1)S(1)} %collective-permute-done.34.rest_5_), channel_id=1, source_target_pairs={{0,1},{1,0},{2,3},{3,2},{4,5},{5,4},{6,7},{7,6},{8,9},{9,8},{10,11... | collective-permute-start | bytes 1474568 | tf_op jit(solution)/shard_map/ppermute | solution.py:164
  (36 other events, 195.4 us)
